TPU v7x, 768 devices: a whole 4x8x12 slice. The times are simulated.
768 devices in a mesh: blk: 24 (over z_lo, x), uly: 32 (over z_hi, y, core).
Axes of the slice: x: 4, y: 8, z: 12 (z_hi: 2, z_lo: 6; z = z_hi * 6 + z_lo), core: 2. Of those that a mesh axis runs over, the one named last changes fastest.
Arguments:
- queries: bfloat16 [98304, 4096], P(('blk', 'uly')), may hold values from -1.5 to 1.5
- keys: bfloat16 [98304, 1024], P(('blk', 'uly')), may hold values from -1.5 to 1.5
- values: bfloat16 [98304, 1024], P(('blk', 'uly')), may hold values from -6 to 6
- grad_out: bfloat16 [98304, 4096], P(('blk', 'uly')), may hold values from -96 to 96
- row_lse: float32 [98304, 32], P('blk', 'uly'), may hold values from 6 to 7.5
- row_delta: float32 [98304, 32], P('blk', 'uly'), may hold values from -960 to 960
- pattern: int32 [768, 2], replicated, may hold values from 0 to 767, as said below
- memory_keys: bfloat16 [128, 4096], P(None, 'uly'), may hold values from -1.5 to 1.5
- memory_values: bfloat16 [128, 4096], P(None, 'uly'), may hold values from -6 to 6
Outputs:
- grad_queries: bfloat16 [98304, 4096], P(('blk', 'uly'))
- grad_keys: float32 [98304, 1024], P(('blk', 'uly'))
- grad_values: float32 [98304, 1024], P(('blk', 'uly'))
- grad_memory_keys: float32 [128, 4096], P(None, 'uly')
- grad_memory_values: float32 [128, 4096], P(None, 'uly')
Inputs may be any that keep to these rules, and one draw needn't show every extreme that they name: `pattern`: query block b lies in span b // 32. The rows of one span name exactly one block of every span that is neither that span nor beside it; all their other named blocks lie in the span itself.
All inputs are finite; a program needn't handle non-finite values.
Results may differ from a plain program's by a relative error of at most 0.0085.
Values may be sent and summed in bfloat16 or wider, within the bound.
A program may use at most 64 MiB of HBM per device.

v0:
```python
import math

import jax
import jax.numpy as jnp
from jax import lax
from jax.sharding import PartitionSpec as P

QUERY_HEADS = 32
KEY_HEADS = 8
HEAD_FEATURES = 128
BLOCK = 128
RANDOM = 2


def shards(
    queries, keys, values, grad_out, row_lse, row_delta, pattern, memory_keys, memory_values
):
    span_count = lax.axis_size("blk")
    head_ways = lax.axis_size("uly")
    my_span = lax.axis_index("blk")
    present_rows = queries.shape[0]
    span_rows = present_rows * head_ways
    block_count = span_rows // BLOCK
    local_heads = QUERY_HEADS // head_ways
    group_width = QUERY_HEADS // KEY_HEADS
    entries = block_count * RANDOM
    score_scale = HEAD_FEATURES ** (-0.5)
    step_blocks = math.gcd(block_count, max(1, 512 // BLOCK))
    step_count = block_count // step_blocks
    pool_blocks = block_count + span_count + 1

    def widen_heads(key_value_rows):
        spread_rows = jnp.broadcast_to(
            key_value_rows.reshape(present_rows, KEY_HEADS, 1, HEAD_FEATURES),
            (present_rows, KEY_HEADS, group_width, HEAD_FEATURES),
        )
        return spread_rows.reshape(present_rows, QUERY_HEADS * HEAD_FEATURES)

    query_x, dout_x = (
        lax.all_to_all(queries, "uly", split_axis=1, concat_axis=0, tiled=True),
        lax.all_to_all(grad_out, "uly", split_axis=1, concat_axis=0, tiled=True),
    )
    key_x, value_x = (
        lax.all_to_all(widen_heads(keys), "uly", split_axis=1, concat_axis=0, tiled=True),
        lax.all_to_all(widen_heads(values), "uly", split_axis=1, concat_axis=0, tiled=True),
    )

    def by_head(wide_rows):
        return wide_rows.reshape(block_count, BLOCK, local_heads, HEAD_FEATURES).transpose(
            2, 0, 1, 3
        )

    def stat_head(stat_rows):
        return stat_rows.reshape(block_count, BLOCK, local_heads).transpose(2, 0, 1)

    query_heads = by_head(query_x)
    key_heads = by_head(key_x)
    value_heads = by_head(value_x)
    dout_heads = by_head(dout_x)
    lse_heads = stat_head(row_lse)
    delta_heads = stat_head(row_delta)
    flat_pattern = pattern.reshape(span_count, entries)
    owner_all = flat_pattern // block_count
    local_all = flat_pattern % block_count
    span_ids = jnp.arange(span_count, dtype=jnp.int32)
    near_span = jnp.abs(span_ids - my_span) == 1
    other_span = span_ids != my_span
    from_me = (owner_all == my_span) & other_span[:, None]
    named_block = jnp.sum(jnp.where(from_me, local_all, 0), axis=1)
    edge_block = jnp.where(span_ids > my_span, block_count - 1, 0)
    send_block = jnp.where(near_span, edge_block, named_block)
    my_pattern = lax.dynamic_slice_in_dim(flat_pattern, my_span, 1, 0)[0]
    my_owner = my_pattern // block_count
    random_index = jnp.where(my_owner == my_span, my_pattern % block_count, block_count + my_owner)
    random_index = random_index.reshape(block_count, RANDOM)
    block_ids = jnp.arange(block_count, dtype=jnp.int32)
    left_index = jnp.where(block_ids > 0, block_ids - 1, block_count + jnp.maximum(my_span - 1, 0))
    right_index = jnp.where(
        block_ids < block_count - 1,
        block_ids + 1,
        block_count + jnp.minimum(my_span + 1, span_count - 1),
    )
    memory_index = jnp.full((block_count, 1), block_count + span_count, jnp.int32)
    pair_index = jnp.concatenate(
        [left_index[:, None], block_ids[:, None], right_index[:, None], random_index, memory_index],
        axis=1,
    )
    left_ok = (block_ids > 0) | (my_span > 0)
    right_ok = (block_ids < block_count - 1) | (my_span < span_count - 1)
    pair_ok = jnp.concatenate(
        [
            left_ok[:, None],
            jnp.ones((block_count, 1), bool),
            right_ok[:, None],
            jnp.ones((block_count, RANDOM + 1), bool),
        ],
        axis=1,
    ).astype(jnp.float32)
    key_send = key_heads[:, send_block]
    value_send = value_heads[:, send_block]
    key_in, value_in = (
        lax.all_to_all(key_send, "blk", split_axis=1, concat_axis=1, tiled=True),
        lax.all_to_all(value_send, "blk", split_axis=1, concat_axis=1, tiled=True),
    )

    def memory_block(memory):
        return memory.reshape(BLOCK, local_heads, HEAD_FEATURES).transpose(1, 0, 2)[:, None]

    key_pool = jnp.concatenate([key_heads, key_in, memory_block(memory_keys)], axis=1)
    value_pool = jnp.concatenate([value_heads, value_in, memory_block(memory_values)], axis=1)

    def one_step(totals, step_id):
        key_acc, value_acc = totals
        first_block = step_id * step_blocks

        def take_part(array):
            return lax.dynamic_slice_in_dim(array, first_block, step_blocks, 1)

        query_part = take_part(query_heads)
        dout_part = take_part(dout_heads)
        lse_part = take_part(lse_heads)
        delta_part = take_part(delta_heads)
        index_part = lax.dynamic_slice_in_dim(pair_index, first_block, step_blocks, 0)
        valid_part = lax.dynamic_slice_in_dim(pair_ok, first_block, step_blocks, 0)
        key_sets = key_pool[:, index_part]
        value_sets = value_pool[:, index_part]
        scores = (
            jnp.einsum(
                "hnad,hnskd->hnsak", query_part, key_sets, preferred_element_type=jnp.float32
            )
            * score_scale
        )
        weights = (
            jnp.exp(scores - lse_part[:, :, None, :, None]) * valid_part[None, :, :, None, None]
        )
        dweights = jnp.einsum(
            "hnad,hnskd->hnsak", dout_part, value_sets, preferred_element_type=jnp.float32
        )
        dscores = weights * (dweights - delta_part[:, :, None, :, None])
        weight_bf = weights.astype(jnp.bfloat16)
        dscore_bf = dscores.astype(jnp.bfloat16)
        grad_q_part = (
            jnp.einsum("hnsak,hnskd->hnad", dscore_bf, key_sets, preferred_element_type=jnp.float32)
            * score_scale
        ).astype(jnp.bfloat16)
        key_term = (
            jnp.einsum(
                "hnsak,hnad->hnskd", dscore_bf, query_part, preferred_element_type=jnp.float32
            )
            * score_scale
        ).astype(jnp.bfloat16)
        value_term = jnp.einsum(
            "hnsak,hnad->hnskd", weight_bf, dout_part, preferred_element_type=jnp.float32
        ).astype(jnp.bfloat16)
        key_acc = key_acc.at[:, index_part].add(key_term.astype(jnp.float32))
        value_acc = value_acc.at[:, index_part].add(value_term.astype(jnp.float32))
        return ((key_acc, value_acc), grad_q_part)

    empty_pool = jnp.zeros((local_heads, pool_blocks, BLOCK, HEAD_FEATURES), jnp.float32)
    (key_acc, value_acc), grad_q_steps = lax.scan(
        one_step, (empty_pool, empty_pool), jnp.arange(step_count, dtype=jnp.int32)
    )
    grad_q = grad_q_steps.transpose(1, 0, 2, 3, 4).reshape(
        local_heads, block_count, BLOCK, HEAD_FEATURES
    )
    grad_k_local = key_acc[:, :block_count]
    grad_v_local = value_acc[:, :block_count]
    memory_dk = key_acc[:, block_count + span_count]
    memory_dv = value_acc[:, block_count + span_count]
    key_slots = key_acc[:, block_count : block_count + span_count].astype(jnp.bfloat16)
    value_slots = value_acc[:, block_count : block_count + span_count].astype(jnp.bfloat16)
    key_back, value_back = (
        lax.all_to_all(key_slots, "blk", split_axis=1, concat_axis=1, tiled=True),
        lax.all_to_all(value_slots, "blk", split_axis=1, concat_axis=1, tiled=True),
    )
    grad_k_local = grad_k_local.at[:, send_block].add(key_back.astype(jnp.float32))
    grad_v_local = grad_v_local.at[:, send_block].add(value_back.astype(jnp.float32))

    def to_rows(head_blocks):
        return head_blocks.transpose(1, 2, 0, 3).reshape(span_rows, local_heads * HEAD_FEATURES)

    grad_q_rows = lax.all_to_all(to_rows(grad_q), "uly", split_axis=0, concat_axis=1, tiled=True)
    grad_k_rows, grad_v_rows = (
        lax.all_to_all(
            to_rows(grad_k_local.astype(jnp.bfloat16)),
            "uly",
            split_axis=0,
            concat_axis=1,
            tiled=True,
        ),
        lax.all_to_all(
            to_rows(grad_v_local.astype(jnp.bfloat16)),
            "uly",
            split_axis=0,
            concat_axis=1,
            tiled=True,
        ),
    )

    def group_sum(rows_by_head):
        summed_terms = jnp.sum(
            rows_by_head.astype(jnp.float32).reshape(
                present_rows, KEY_HEADS, group_width, HEAD_FEATURES
            ),
            axis=2,
        )
        return summed_terms.reshape(present_rows, KEY_HEADS * HEAD_FEATURES)

    def memory_rows(memory_terms):
        return memory_terms.transpose(1, 0, 2).reshape(BLOCK, local_heads * HEAD_FEATURES)

    memory_keys_total, memory_values_total = lax.psum(
        (memory_rows(memory_dk), memory_rows(memory_dv)), "blk"
    )
    return (
        grad_q_rows,
        group_sum(grad_k_rows),
        group_sum(grad_v_rows),
        memory_keys_total,
        memory_values_total,
    )


def solution(mesh):
    in_specs = (
        P(("blk", "uly"), None),
        P(("blk", "uly"), None),
        P(("blk", "uly"), None),
        P(("blk", "uly"), None),
        P("blk", "uly"),
        P("blk", "uly"),
        P(),
        P(None, "uly"),
        P(None, "uly"),
    )
    out_specs = (
        P(("blk", "uly"), None),
        P(("blk", "uly"), None),
        P(("blk", "uly"), None),
        P(None, "uly"),
        P(None, "uly"),
    )
    return jax.shard_map(shards, mesh=mesh, in_specs=in_specs, out_specs=out_specs, check_vma=False)
```

profile of v0, /device:TPU:8, one launch (start us, length us, event | category | flops | bytes accessed | tf_op | source)
XLA Modules:
  0.0 990.9 jit_solution(8012883311162971904)
XLA Ops:
  9.4 20.4 %all-to-all-start.3 = ((bf16[128,32,128]{2,0,1:T(8,128)(2,1)}), bf16[128,32,128]{2,0,1:T(8,128)(2,1)S(1)}, u32[]{:S(2)}, u32[]{:S(2)}) async-start(bf16[128,32,128]{2,0,1:T(8,128)(2,1)} %bitcast.42), calls=%async_computation.3 | async-start | bytes 2097152 | tf_op jit(solution)/shard_map/all_to_all | solution.py:45
  29.8 27.6 %all-to-all-done.3 = bf16[128,32,128]{2,0,1:T(8,128)(2,1)S(1)} async-done(((bf16[128,32,128]{2,0,1:T(8,128)(2,1)}), bf16[128,32,128]{2,0,1:T(8,128)(2,1)S(1)}, u32[]{:S(2)}, u32[]{:S(2)}) %all-to-all-start.3) | async-done | bytes 1048608 | tf_op jit(solution)/shard_map/all_to_all | solution.py:45
  58.7 11.2 %all-to-all-start = ((bf16[128,32,128]{2,0,1:T(8,128)(2,1)}), bf16[128,32,128]{2,0,1:T(8,128)(2,1)S(1)}, u32[]{:S(2)}, u32[]{:S(2)}) async-start(bf16[128,32,128]{2,0,1:T(8,128)(2,1)} %bitcast.30), calls=%async_computation | async-start | bytes 2097152 | tf_op jit(solution)/shard_map/all_to_all | solution.py:44
  71.2 26.2 %all-to-all-done = bf16[128,32,128]{2,0,1:T(8,128)(2,1)S(1)} async-done(((bf16[128,32,128]{2,0,1:T(8,128)(2,1)}), bf16[128,32,128]{2,0,1:T(8,128)(2,1)S(1)}, u32[]{:S(2)}, u32[]{:S(2)}) %all-to-all-start) | async-done | bytes 1048608 | tf_op jit(solution)/shard_map/all_to_all | solution.py:44
  97.5 11.9 %all-to-all-start.2 = ((bf16[128,32,128]{0,2,1:T(8,128)(2,1)}), bf16[128,32,128]{0,2,1:T(8,128)(2,1)S(1)}, u32[]{:S(2)}, u32[]{:S(2)}) async-start(bf16[128,32,128]{0,2,1:T(8,128)(2,1)} %bitcast.222), calls=%async_computation.2 | async-start | bytes 2097152 | tf_op jit(solution)/shard_map/all_to_all | solution.py:40
  111.4 25.5 %all-to-all-done.2 = bf16[128,32,128]{0,2,1:T(8,128)(2,1)S(1)} async-done(((bf16[128,32,128]{0,2,1:T(8,128)(2,1)}), bf16[128,32,128]{0,2,1:T(8,128)(2,1)S(1)}, u32[]{:S(2)}, u32[]{:S(2)}) %all-to-all-start.2) | async-done | bytes 1048608 | tf_op jit(solution)/shard_map/all_to_all | solution.py:40
  136.9 43.8 %all-to-all-start.4 = ((bf16[1,24,128,128]{3,2,0,1:T(8,128)(2,1)}), bf16[1,24,128,128]{3,2,0,1:T(8,128)(2,1)}, u32[]{:S(2)}, u32[]{:S(2)}) async-start(bf16[1,24,128,128]{3,2,0,1:T(8,128)(2,1)} %bitcast.224), calls=%async_computation.4 | async-start | bytes 1572864 | tf_op jit(solution)/shard_map/all_to_all | solution.py:103
  182.3 30.0 %all-to-all-done.4 = bf16[1,24,128,128]{3,2,0,1:T(8,128)(2,1)} async-done(((bf16[1,24,128,128]{3,2,0,1:T(8,128)(2,1)}), bf16[1,24,128,128]{3,2,0,1:T(8,128)(2,1)}, u32[]{:S(2)}, u32[]{:S(2)}) %all-to-all-start.4) | async-done | bytes 786464 | tf_op jit(solution)/shard_map/all_to_all | solution.py:103
  220.0 28.5 %all-to-all-done.1 = bf16[1,24,128,128]{3,2,0,1:T(8,128)(2,1)} async-done(((bf16[1,24,128,128]{3,2,0,1:T(8,128)(2,1)}), bf16[1,24,128,128]{3,2,0,1:T(8,128)(2,1)}, u32[]{:S(2)}, u32[]{:S(2)}) %all-to-all-start.1) | async-done | bytes 786464 | tf_op jit(solution)/shard_map/all_to_all | solution.py:102
  248.6 7.0 all-to-all-start.5
  263.8 31.1 %all-to-all-done.5 = bf16[128,32,128]{0,2,1:T(8,128)(2,1)} async-done(((bf16[128,32,128]{0,2,1:T(8,128)(2,1)}), bf16[128,32,128]{0,2,1:T(8,128)(2,1)}, u32[]{:S(2)}, u32[]{:S(2)}) %all-to-all-start.5) | async-done | bytes 1048608 | tf_op jit(solution)/shard_map/all_to_all | solution.py:41
  299.5 188.0 %while.14 = (s32[]{:T(128)}, f32[1,57,128,128]{3,2,1,0:T(8,128)}, f32[1,57,128,128]{3,2,1,0:T(8,128)}, bf16[8,1,4,128,128]{4,3,2,1,0:T(8,128)(2,1)}, s32[8]{0:T(...) while((s32[]{:T(128)}, f32[1,57,128,128]{3,2,1,0:T(8,128)}, ...), condition=%wide.region_5.6_spmd, body=%wide.region_2.5_spmd.sunk | while | flops 508953664 | bytes 37375320 | solution.py:160
  311.0 6.1 scatter_fusion.1
  364.0 6.0 scatter_fusion
  451.9 6.1 scatter_fusion.1
  489.9 10.0 %all-to-all-start.9 = ((bf16[1,24,128,128]{3,2,0,1:T(8,128)(2,1)}), bf16[1,24,128,128]{3,2,0,1:T(8,128)(2,1)S(1)}, u32[]{:S(2)}, u32[]{:S(2)}) async-start(bf16[1,24,128,128]{3,2,0,1:T(8,128)(2,1)} %slice.42), calls=%async_computation.9 | async-start | bytes 1572864 | tf_op jit(solution)/shard_map/all_to_all | solution.py:174
  501.5 29.7 %all-to-all-done.9 = bf16[1,24,128,128]{3,2,0,1:T(8,128)(2,1)S(1)} async-done(((bf16[1,24,128,128]{3,2,0,1:T(8,128)(2,1)}), bf16[1,24,128,128]{3,2,0,1:T(8,128)(2,1)S(1)}, u32[]{:S(2)}, u32[]{:S(2)}) %all-to-all-start.9) | async-done | bytes 786464 | tf_op jit(solution)/shard_map/all_to_all | solution.py:174
  531.2 36.1 %all_to_all.129 = bf16[1,24,128,128]{3,2,0,1:T(8,128)(2,1)} all-to-all(bf16[1,24,128,128]{3,2,0,1:T(8,128)(2,1)S(1)} %slice.43), channel_id=1, replica_groups=mesh['blk'=24,'uly'=32] {'blk'}, dimensions={1} | all-to-all | bytes 1572864 | tf_op jit(solution)/shard_map/all_to_all | solution.py:173
  581.8 30.6 %all-to-all-done.6 = bf16[32,128,128]{2,1,0:T(8,128)(2,1)S(1)} async-done(((bf16[32,128,128]{2,1,0:T(8,128)(2,1)}), bf16[32,128,128]{2,1,0:T(8,128)(2,1)S(1)}, u32[]{:S(2)}, u32[]{:S(2)}) %all-to-all-start.6) | async-done | bytes 1048608 | tf_op jit(solution)/shard_map/all_to_all | solution.py:182
  612.4 10.9 %all-to-all-start.8 = ((bf16[32,128,128]{2,1,0:T(8,128)(2,1)}), bf16[32,128,128]{2,1,0:T(8,128)(2,1)}, u32[]{:S(2)}, u32[]{:S(2)}) async-start(bf16[32,128,128]{2,1,0:T(8,128)(2,1)} %convert_element_type.86), calls=%async_computation.8 | async-start | bytes 2097152 | tf_op jit(solution)/shard_map/all_to_all | solution.py:184
  632.3 23.7 %all-to-all-done.8 = bf16[32,128,128]{2,1,0:T(8,128)(2,1)} async-done(((bf16[32,128,128]{2,1,0:T(8,128)(2,1)}), bf16[32,128,128]{2,1,0:T(8,128)(2,1)}, u32[]{:S(2)}, u32[]{:S(2)}) %all-to-all-start.8) | async-done | bytes 1048608 | tf_op jit(solution)/shard_map/all_to_all | solution.py:184
  656.0 10.2 %all-to-all-start.10 = ((bf16[32,128,128]{2,1,0:T(8,128)(2,1)}), bf16[32,128,128]{2,1,0:T(8,128)(2,1)S(1)}, u32[]{:S(2)}, u32[]{:S(2)}) async-start(bf16[32,128,128]{2,1,0:T(8,128)(2,1)} %convert_element_type.87), calls=%async_computation.10 | async-start | bytes 2097152 | tf_op jit(solution)/shard_map/all_to_all | solution.py:191
  673.9 22.4 %all-to-all-done.10 = bf16[32,128,128]{2,1,0:T(8,128)(2,1)S(1)} async-done(((bf16[32,128,128]{2,1,0:T(8,128)(2,1)}), bf16[32,128,128]{2,1,0:T(8,128)(2,1)S(1)}, u32[]{:S(2)}, u32[]{:S(2)}) %all-to-all-start.10) | async-done | bytes 1048608 | tf_op jit(solution)/shard_map/all_to_all | solution.py:191
  697.6 283.5 %all-reduce.3.cloned.1.call-done = (f32[128,128]{1,0:T(8,128)}, f32[128,128]{1,0:T(8,128)}) async-done(((f32[128,128]{1,0:T(8,128)}, f32[128,128]{1,0:T(8,128)}), (f32[128,128]{1,0:T(8,128)}, f32[128,128]{1,0:T(8,128)})) %all-reduce.3.cloned.1.call-update) | async-done | bytes 131088 | tf_op jit(solution)/shard_map/psum | solution.py:212
  (248 shorter events, 232.0 us)
Async XLA Ops:
  7.2 22.6 %copy-start.7 = (bf16[128,1024]{1,0:T(8,128)(2,1)S(1)}, bf16[128,1024]{1,0:T(8,128)(2,1)}, u32[]{:S(2)}) copy-start(bf16[128,1024]{1,0:T(8,128)(2,1)} %param.12) | copy-start | bytes 786436
  9.4 48.1 %all-to-all-start.3 = ((bf16[128,32,128]{2,0,1:T(8,128)(2,1)}), bf16[128,32,128]{2,0,1:T(8,128)(2,1)S(1)}, u32[]{:S(2)}, u32[]{:S(2)}) async-start(bf16[128,32,128]{2,0,1:T(8,128)(2,1)} %bitcast.42), calls=%async_computation.3 | async-start | bytes 2097152 | tf_op jit(solution)/shard_map/all_to_all | solution.py:45
  29.8 40.1 %copy-start.6 = (bf16[128,4096]{1,0:T(8,128)(2,1)S(1)}, bf16[128,4096]{1,0:T(8,128)(2,1)}, u32[]{:S(2)}) copy-start(bf16[128,4096]{1,0:T(8,128)(2,1)} %param.11) | copy-start | bytes 3145732
  58.7 38.8 %all-to-all-start = ((bf16[128,32,128]{2,0,1:T(8,128)(2,1)}), bf16[128,32,128]{2,0,1:T(8,128)(2,1)S(1)}, u32[]{:S(2)}, u32[]{:S(2)}) async-start(bf16[128,32,128]{2,0,1:T(8,128)(2,1)} %bitcast.30), calls=%async_computation | async-start | bytes 2097152 | tf_op jit(solution)/shard_map/all_to_all | solution.py:44
  69.9 39.6 %copy-start.10 = (s32[768,2]{0,1:T(2,128)S(1)}, s32[768,2]{0,1:T(2,128)}, u32[]{:S(2)}) copy-start(s32[768,2]{0,1:T(2,128)} %param.17) | copy-start | bytes 18436
  97.5 39.4 %all-to-all-start.2 = ((bf16[128,32,128]{0,2,1:T(8,128)(2,1)}), bf16[128,32,128]{0,2,1:T(8,128)(2,1)S(1)}, u32[]{:S(2)}, u32[]{:S(2)}) async-start(bf16[128,32,128]{0,2,1:T(8,128)(2,1)} %bitcast.222), calls=%async_computation.2 | async-start | bytes 2097152 | tf_op jit(solution)/shard_map/all_to_all | solution.py:40
  136.9 75.4 %all-to-all-start.4 = ((bf16[1,24,128,128]{3,2,0,1:T(8,128)(2,1)}), bf16[1,24,128,128]{3,2,0,1:T(8,128)(2,1)}, u32[]{:S(2)}, u32[]{:S(2)}) async-start(bf16[1,24,128,128]{3,2,0,1:T(8,128)(2,1)} %bitcast.224), calls=%async_computation.4 | async-start | bytes 1572864 | tf_op jit(solution)/shard_map/all_to_all | solution.py:103
  212.3 36.3 %all-to-all-start.1 = ((bf16[1,24,128,128]{3,2,0,1:T(8,128)(2,1)}), bf16[1,24,128,128]{3,2,0,1:T(8,128)(2,1)}, u32[]{:S(2)}, u32[]{:S(2)}) async-start(bf16[1,24,128,128]{3,2,0,1:T(8,128)(2,1)} %bitcast.225), calls=%async_computation.1 | async-start | bytes 1572864 | tf_op jit(solution)/shard_map/all_to_all | solution.py:102
  220.0 38.5 %copy-start.8 = (bf16[128,128]{1,0:T(8,128)(2,1)S(1)}, bf16[128,128]{1,0:T(8,128)(2,1)}, u32[]{:S(2)}) copy-start(bf16[128,128]{1,0:T(8,128)(2,1)} %param.19) | copy-start | bytes 98308
  248.6 46.3 %all-to-all-start.5 = ((bf16[128,32,128]{0,2,1:T(8,128)(2,1)}), bf16[128,32,128]{0,2,1:T(8,128)(2,1)}, u32[]{:S(2)}, u32[]{:S(2)}) async-start(bf16[128,32,128]{0,2,1:T(8,128)(2,1)} %bitcast.221), calls=%async_computation.5 | async-start | bytes 2097152 | tf_op jit(solution)/shard_map/all_to_all | solution.py:41
  299.5 10.7 %copy-start.1 = (bf16[1,32,128,128]{2,3,1,0:T(8,128)(2,1)}, bf16[1,32,128,128]{2,3,1,0:T(8,128)(2,1)S(1)}, u32[]{:S(2)}) copy-start(bf16[1,32,128,128]{2,3,1,0:T(8,128)(2,1)S(1)} %get-tuple-element.297) | copy-start | bytes 3145732 | tf_op jit(solution)/shard_map/while
  323.0 10.7 %copy-start.1 = (bf16[1,32,128,128]{2,3,1,0:T(8,128)(2,1)}, bf16[1,32,128,128]{2,3,1,0:T(8,128)(2,1)S(1)}, u32[]{:S(2)}) copy-start(bf16[1,32,128,128]{2,3,1,0:T(8,128)(2,1)S(1)} %get-tuple-element.297) | copy-start | bytes 3145732 | tf_op jit(solution)/shard_map/while
  346.5 10.7 %copy-start.1 = (bf16[1,32,128,128]{2,3,1,0:T(8,128)(2,1)}, bf16[1,32,128,128]{2,3,1,0:T(8,128)(2,1)S(1)}, u32[]{:S(2)}) copy-start(bf16[1,32,128,128]{2,3,1,0:T(8,128)(2,1)S(1)} %get-tuple-element.297) | copy-start | bytes 3145732 | tf_op jit(solution)/shard_map/while
  370.0 10.7 %copy-start.1 = (bf16[1,32,128,128]{2,3,1,0:T(8,128)(2,1)}, bf16[1,32,128,128]{2,3,1,0:T(8,128)(2,1)S(1)}, u32[]{:S(2)}) copy-start(bf16[1,32,128,128]{2,3,1,0:T(8,128)(2,1)S(1)} %get-tuple-element.297) | copy-start | bytes 3145732 | tf_op jit(solution)/shard_map/while
  393.5 10.7 %copy-start.1 = (bf16[1,32,128,128]{2,3,1,0:T(8,128)(2,1)}, bf16[1,32,128,128]{2,3,1,0:T(8,128)(2,1)S(1)}, u32[]{:S(2)}) copy-start(bf16[1,32,128,128]{2,3,1,0:T(8,128)(2,1)S(1)} %get-tuple-element.297) | copy-start | bytes 3145732 | tf_op jit(solution)/shard_map/while
  417.0 10.7 %copy-start.1 = (bf16[1,32,128,128]{2,3,1,0:T(8,128)(2,1)}, bf16[1,32,128,128]{2,3,1,0:T(8,128)(2,1)S(1)}, u32[]{:S(2)}) copy-start(bf16[1,32,128,128]{2,3,1,0:T(8,128)(2,1)S(1)} %get-tuple-element.297) | copy-start | bytes 3145732 | tf_op jit(solution)/shard_map/while
  440.4 10.7 %copy-start.1 = (bf16[1,32,128,128]{2,3,1,0:T(8,128)(2,1)}, bf16[1,32,128,128]{2,3,1,0:T(8,128)(2,1)S(1)}, u32[]{:S(2)}) copy-start(bf16[1,32,128,128]{2,3,1,0:T(8,128)(2,1)S(1)} %get-tuple-element.297) | copy-start | bytes 3145732 | tf_op jit(solution)/shard_map/while
  463.9 10.7 %copy-start.1 = (bf16[1,32,128,128]{2,3,1,0:T(8,128)(2,1)}, bf16[1,32,128,128]{2,3,1,0:T(8,128)(2,1)S(1)}, u32[]{:S(2)}) copy-start(bf16[1,32,128,128]{2,3,1,0:T(8,128)(2,1)S(1)} %get-tuple-element.297) | copy-start | bytes 3145732 | tf_op jit(solution)/shard_map/while
  489.9 41.3 %all-to-all-start.9 = ((bf16[1,24,128,128]{3,2,0,1:T(8,128)(2,1)}), bf16[1,24,128,128]{3,2,0,1:T(8,128)(2,1)S(1)}, u32[]{:S(2)}, u32[]{:S(2)}) async-start(bf16[1,24,128,128]{3,2,0,1:T(8,128)(2,1)} %slice.42), calls=%async_computation.9 | async-start | bytes 1572864 | tf_op jit(solution)/shard_map/all_to_all | solution.py:174
  531.2 36.1 %copy-start.3 = (bf16[1,24,128,128]{3,2,0,1:T(8,128)(2,1)}, bf16[1,24,128,128]{3,2,0,1:T(8,128)(2,1)S(1)}, u32[]{:S(2)}) copy-start(bf16[1,24,128,128]{3,2,0,1:T(8,128)(2,1)S(1)} %all-to-all-done.9) | copy-start | bytes 2359300
  567.3 45.1 %all-to-all-start.6 = ((bf16[32,128,128]{2,1,0:T(8,128)(2,1)}), bf16[32,128,128]{2,1,0:T(8,128)(2,1)S(1)}, u32[]{:S(2)}, u32[]{:S(2)}) async-start(bf16[32,128,128]{2,1,0:T(8,128)(2,1)} %bitcast.228), calls=%async_computation.6 | async-start | bytes 2097152 | tf_op jit(solution)/shard_map/all_to_all | solution.py:182
  612.4 43.6 %all-to-all-start.8 = ((bf16[32,128,128]{2,1,0:T(8,128)(2,1)}), bf16[32,128,128]{2,1,0:T(8,128)(2,1)}, u32[]{:S(2)}, u32[]{:S(2)}) async-start(bf16[32,128,128]{2,1,0:T(8,128)(2,1)} %convert_element_type.86), calls=%async_computation.8 | async-start | bytes 2097152 | tf_op jit(solution)/shard_map/all_to_all | solution.py:184
  656.0 40.3 %all-to-all-start.10 = ((bf16[32,128,128]{2,1,0:T(8,128)(2,1)}), bf16[32,128,128]{2,1,0:T(8,128)(2,1)S(1)}, u32[]{:S(2)}, u32[]{:S(2)}) async-start(bf16[32,128,128]{2,1,0:T(8,128)(2,1)} %convert_element_type.87), calls=%async_computation.10 | async-start | bytes 2097152 | tf_op jit(solution)/shard_map/all_to_all | solution.py:191
  666.3 314.8 %all-reduce.3.cloned.1.call-start = ((), (), s32[]{:S(2)}) async-start(), calls=%async_computation.11 | async-start | bytes 262144 | tf_op jit(solution)/shard_map/psum | solution.py:212
  (12 other events, 55.1 us)
Sparse Core Ops, SparseCore 0:
  671.0 310.0 all-reduce.2
where the time goes:
time: 996 us; the launch traced here: 991 us
  waiting for transfers between devices  559 us (56%)
  starting transfers between devices  137 us (14%)
  other arithmetic  121 us (12%)
  local copies, waits for them, and re-layouts  82.7 us (8%)
  blocking collectives  36.1 us (4%)
  matrix products  35.6 us (4%)
  between operations  14.4 us (1%)
    psum x1, waiting for transfers between devices, shards(): lax.psum((memory_rows(memory_dk), memory_rows(memory_dv)), 'blk')  283 us
    scatter-add x8, other arithmetic, one_step(): value_acc = value_acc.at[:, index_part].add(value_term.astype(jnp.float32))  48 us
    scatter-add x8, other arithmetic, one_step(): key_acc = key_acc.at[:, index_part].add(key_term.astype(jnp.float32))  47.8 us
    all_to_all x1, starting transfers between devices, shards(): lax.all_to_all(value_send, 'blk', split_axis=1, concat_axis=1, tiled=True)  43.8 us
    all_to_all x1, blocking collectives, shards(): lax.all_to_all(key_slots, 'blk', split_axis=1, concat_axis=1, tiled=True)  36.1 us
    all_to_all x1, waiting for transfers between devices, shards(): lax.all_to_all(grad_out, 'uly', split_axis=1, concat_axis=0, tiled=True)  31.1 us
    all_to_all x1, waiting for transfers between devices, shards(): lax.all_to_all(to_rows(grad_q), 'uly', split_axis=0, concat_axis=1, tiled...  30.6 us
    all_to_all x1, waiting for transfers between devices, shards(): lax.all_to_all(value_send, 'blk', split_axis=1, concat_axis=1, tiled=True)  30 us
  transfers between devices with their start and end apart: 11, of which 11 were waited for; matrix products, arithmetic and copies ran while one was open for 4% of the time, Pallas kernels for 0%

commit v1 on v0

v1 whole, which is shorter than its diff:
```python
import functools

import jax
import jax.numpy as jnp
from jax import lax
from jax.experimental import pallas as pl
from jax.experimental.pallas import tpu as pltpu
from jax.sharding import PartitionSpec as P

QUERY_HEADS = 32
KEY_HEADS = 8
FEATURES = 128
BLOCK = 128
RANDOM = 2
SLOTS = 3 + RANDOM
SCALE = FEATURES ** (-0.5)
MESH = pl.DeviceIdType.MESH

SPANS, PLACES = 24, 32
HALF = PLACES // 2
YS = HALF // 2
X, Z = 4, 6
PARTS = 8
ROWS = 4 * BLOCK // PARTS

F32, BF16 = jnp.float32, jnp.bfloat16


def position():
    s, u = lax.axis_index("blk"), lax.axis_index("uly")
    return s, u, u // HALF, u % HALF, u % 2


def far_place(s, u, t):
    a, b = s // X, t // X
    d = (b - a + Z) % Z
    even = (s % X + t % X) % 2 == 0
    three = jnp.where((a < Z // 2) == even, Z // 2, -(Z // 2))
    step = jnp.where(d == Z // 2, three, jnp.where(d < Z // 2, d, d - Z))
    z = ((u // HALF) * Z + a + step + 2 * Z) % (2 * Z)
    return (z // Z) * HALF + u % HALF


def remote(src, dst, sent, got, blk, uly):
    return pltpu.make_async_remote_copy(
        src_ref=src, dst_ref=dst, send_sem=sent, recv_sem=got, device_id=(blk, uly), device_id_type=MESH
    )


def send(src, dst, sent, got, blk, uly, here):
    @pl.when(jnp.logical_not(here))
    def _():
        remote(src, dst, sent, got, blk, uly).start()

    @pl.when(here)
    def _():
        pltpu.make_async_copy(src, dst, got).start()


def wait(ref, sem):
    pltpu.make_async_copy(ref, ref, sem).wait()


def loop(n, body):
    def step(i, carry):
        body(i)
        return carry

    lax.fori_loop(0, n, step, 0)


def greet(blk, uly):
    pl.semaphore_signal(pltpu.get_barrier_semaphore(), inc=1, device_id=(blk, uly), device_id_type=MESH)


def others(n, me, body):
    def step(i):
        @pl.when(i != me)
        def _():
            body(i)

    loop(n, step)


def gather(
    send_ref, q_ref, do_ref, k_ref, v_ref, stat_ref, mem_ref,
    qh_ref, doh_ref, own_ref, other_ref, far_ref, far_other_ref, stat_out, mem_out,
    out_ref, s_kv, r_kv, s_q, r_q, s_do, r_do, s_z, r_z, s_core, r_core, s_far, r_far, s_stat, r_stat, s_mem, r_mem,
):
    s, u, half, p_me, core = position()
    others(PLACES, u, lambda p: greet(s, p))
    others(SPANS, s, lambda t: greet(t, far_place(s, u, t)))
    pl.semaphore_wait(pltpu.get_barrier_semaphore(), PLACES - 1 + SPANS - 1)

    def columns(ref, i, width):
        return ref.at[:, pl.ds(pl.multiple_of(i * width, width), width)]

    first = half * HALF

    def kv_to(y):
        for kind, ref in ((0, k_ref), (1, v_ref)):
            place = first + 2 * y + kind
            send(columns(ref, y, FEATURES), own_ref.at[first + p_me], s_kv, r_kv, s, place, place == u)

    loop(YS, kv_to)
    for z in range(2):
        place = z * HALF + u // 2
        send(stat_ref.at[z], stat_out.at[u % 2], s_stat.at[z], r_stat, s, place, place == u)
        send(mem_ref, mem_out.at[u % 2], s_mem.at[z], r_mem, s, place, place == u)

    mine = own_ref.at[pl.ds(first, HALF)]
    wait(mine, r_kv)
    swap = remote(mine, mine, s_z, r_z, s, (u + HALF) % PLACES)
    swap.start()
    core_peer = u + 1 - 2 * core
    onward = remote(mine, other_ref.at[pl.ds(first, HALF)], s_core.at[0], r_core.at[0], s, core_peer)
    onward.start()

    def q_to(p):
        here = p == p_me
        send(columns(q_ref, p, 2 * FEATURES), qh_ref.at[p_me], s_q, r_q, s, first + p, here)
        send(columns(do_ref, p, 2 * FEATURES), doh_ref.at[p_me], s_do, r_do, s, first + p, here)

    loop(HALF, q_to)
    second = HALF - first
    theirs = own_ref.at[pl.ds(second, HALF)]
    wait(theirs, r_z)
    onward2 = remote(theirs, other_ref.at[pl.ds(second, HALF)], s_core.at[1], r_core.at[1], s, core_peer)
    onward2.start()

    def far_to(t):
        out_ref[t] = own_ref[send_ref[t]]
        remote(out_ref.at[t], far_ref.at[s], s_far, r_far, t, far_place(s, u, t)).start()

    others(SPANS, s, far_to)
    wait(far_ref.at[pl.ds(0, SPANS - 1)], r_far)
    onward3 = remote(far_ref, far_other_ref, s_core.at[2], r_core.at[2], s, core_peer)
    onward3.start()
    wait(qh_ref, r_q)
    wait(doh_ref, r_do)
    wait(stat_out, r_stat)
    wait(mem_out, r_mem)
    onward.wait_recv()
    onward2.wait_recv()
    onward3.wait_recv()
    wait(own_ref.at[pl.ds(0, HALF - 1)], s_kv)
    wait(qh_ref.at[pl.ds(0, HALF - 1)], s_q)
    wait(doh_ref.at[pl.ds(0, HALF - 1)], s_do)
    wait(out_ref.at[pl.ds(0, SPANS - 1)], s_far)
    swap.wait_send()
    onward.wait_send()
    onward2.wait_send()
    onward3.wait_send()
    for z in range(2):
        @pl.when(z * HALF + u // 2 != u)
        def _():
            wait(stat_out.at[0], s_stat.at[z])
            wait(mem_out.at[0], s_mem.at[z])


def vmem(n):
    return [pl.BlockSpec(memory_space=pltpu.VMEM)] * n


def hbm(n):
    return [pl.BlockSpec(memory_space=pl.ANY)] * n


SMEM = pl.BlockSpec(memory_space=pltpu.SMEM)
DMA = pltpu.SemaphoreType.DMA


def shape(*dims, dtype=BF16):
    return jax.ShapeDtypeStruct(dims, dtype)


def gather_call(sends, q, do, k, v, stats, mem):
    tile = (BLOCK, FEATURES)
    return pl.pallas_call(
        gather,
        in_specs=[SMEM] + hbm(6),
        out_specs=vmem(8),
        out_shape=[
            shape(HALF, BLOCK, 2 * FEATURES), shape(HALF, BLOCK, 2 * FEATURES),
            shape(PLACES, *tile), shape(PLACES, *tile), shape(SPANS, *tile), shape(SPANS, *tile),
            shape(2, 2, HALF, BLOCK, dtype=F32), shape(2, 2, *tile),
        ],
        scratch_shapes=[pltpu.VMEM((SPANS,) + tile, BF16)]
        + [DMA] * 8
        + [DMA((3,)), DMA((3,)), DMA, DMA, DMA((2,)), DMA, DMA((2,)), DMA],
        compiler_params=pltpu.CompilerParams(collective_id=0, has_side_effects=True),
        name="gather",
    )(sends, q, do, k, v, stats, mem)


def attend(
    meta_ref, idx_ref, q_ref, do_ref, stat_ref, own_ref, other_ref, far_ref, far_other_ref, mem_ref,
    gq_ref, keep_ref, give_ref, dmem_ref, pool_ref, acc_ref, macc_ref,
):
    step = pl.program_id(0)
    steps = pl.num_programs(0)
    core = meta_ref[0]

    @pl.when(step == 0)
    def _():
        acc_ref[...] = jnp.zeros_like(acc_ref)
        macc_ref[...] = jnp.zeros_like(macc_ref)

        @pl.loop(0, PLACES)
        def _(n):
            pool_ref[core, n] = own_ref[n]
            pool_ref[1 - core, n] = other_ref[n]

        @pl.loop(0, SPANS)
        def _(n):
            pool_ref[core, PLACES + n] = far_ref[n]
            pool_ref[1 - core, PLACES + n] = far_other_ref[n]

    def dot(a, b, i, j):
        return lax.dot_general(a, b, (((i,), (j,)), ((), ())), preferred_element_type=F32)

    q = [q_ref[0, :, FEATURES * i : FEATURES * (i + 1)] for i in range(2)]
    do = [do_ref[0, :, FEATURES * i : FEATURES * (i + 1)] for i in range(2)]
    q2 = jnp.concatenate(q, axis=0)
    do2 = jnp.concatenate(do, axis=0)
    lse, delta = [
        jnp.concatenate([stat_ref[i, kind, pl.ds(step, 1), :] for i in range(2)], axis=1) for kind in range(2)
    ]
    which = [idx_ref[step, j] for j in range(SLOTS)]
    keys = jnp.concatenate([pool_ref[0, w] for w in which], axis=0)
    values = jnp.concatenate([pool_ref[1, w] for w in which], axis=0)

    weights = jnp.exp(dot(keys, q2, 1, 1) * SCALE - lse)
    dscores = weights * (dot(values, do2, 1, 1) - delta)
    row = lax.broadcasted_iota(jnp.int32, (SLOTS * BLOCK, 1), 0)
    left, right = idx_ref[step, SLOTS], idx_ref[step, SLOTS + 1]
    keep = ((row >= BLOCK) | (left > 0)) & ((row < 2 * BLOCK) | (row >= 3 * BLOCK) | (right > 0))
    weight_bf = jnp.where(keep, weights, 0.0).astype(BF16)
    dscore_bf = jnp.where(keep, dscores, 0.0).astype(BF16)
    dkey = dot(dscore_bf, q2, 1, 0)
    dvalue = dot(weight_bf, do2, 1, 0)
    dquery = dot(dscore_bf, keys, 0, 0)
    for j in range(SLOTS):
        rows = slice(BLOCK * j, BLOCK * (j + 1))
        acc_ref[0, which[j]] += dkey[rows]
        acc_ref[1, which[j]] += dvalue[rows]

    for i in range(2):
        cols = slice(FEATURES * i, FEATURES * (i + 1))
        w = jnp.exp(dot(mem_ref[i, 0], q[i], 1, 1) * SCALE - lse[:, cols])
        ds = (w * (dot(mem_ref[i, 1], do[i], 1, 1) - delta[:, cols])).astype(BF16)
        macc_ref[i, 0] += dot(ds, q[i], 1, 0)
        macc_ref[i, 1] += dot(w.astype(BF16), do[i], 1, 0)
        gq = dquery[BLOCK * i : BLOCK * (i + 1)] + dot(ds, mem_ref[i, 0], 0, 0)
        gq_ref[0, :, cols] = (gq * SCALE).astype(BF16)

    @pl.when(step == steps - 1)
    def _():
        mine = jnp.where(core == 0, SCALE, 1.0)
        theirs = jnp.where(core == 0, 1.0, SCALE)

        @pl.loop(0, PLACES + SPANS)
        def _(n):
            keep_ref[n] = (acc_ref[core, n] * mine).astype(BF16)
            give_ref[n] = (acc_ref[1 - core, n] * theirs).astype(BF16)

        for i in range(2):
            dmem_ref[i, 0] = macc_ref[i, 0] * SCALE
            dmem_ref[i, 1] = macc_ref[i, 1]


def attend_call(meta, idx, q, do, stats, own, other, far, far_other, mem):
    tile = (BLOCK, FEATURES)
    pool = PLACES + SPANS

    def per_block():
        return pl.BlockSpec((1, BLOCK, 2 * FEATURES), lambda b, *_: (b, 0, 0))

    def whole(dims):
        return pl.BlockSpec(dims, lambda b, *_: (0,) * len(dims))

    return pl.pallas_call(
        attend,
        grid_spec=pltpu.PrefetchScalarGridSpec(
            num_scalar_prefetch=2,
            grid=(HALF,),
            in_specs=[per_block(), per_block()] + [whole(a.shape) for a in (stats, own, other, far, far_other, mem)],
            out_specs=[per_block(), whole((pool,) + tile), whole((pool,) + tile), whole((2, 2) + tile)],
            scratch_shapes=[
                pltpu.VMEM((2, pool) + tile, BF16),
                pltpu.VMEM((2, pool) + tile, F32),
                pltpu.VMEM((2, 2) + tile, F32),
            ],
        ),
        out_shape=[
            shape(HALF, BLOCK, 2 * FEATURES), shape(pool, *tile), shape(pool, *tile), shape(2, 2, *tile, dtype=F32),
        ],
        name="attend",
    )(meta, idx, q, do, stats, own, other, far, far_other, mem)


def part_peer(s, r):
    return ((s // X) // 2 * 2 + r % 2) * X + r // 2


def my_part(s):
    return s % X * 2 + s // X % 2


def give_back(
    keep_ref, give_ref, dmem_ref, total_ref, back_ref, part_ref,
    got_ref, out_ref, parts_ref, s_core, r_core, s_far, r_far, s_part, r_part,
):
    s, u, half, p_me, core = position()
    core_peer = u + 1 - 2 * core
    r_me = my_part(s)
    greet(s, core_peer)
    others(SPANS, s, lambda t: greet(t, far_place(s, u, t)))
    others(PARTS, r_me, lambda r: greet(part_peer(s, r), u))
    pl.semaphore_wait(pltpu.get_barrier_semaphore(), 1 + SPANS - 1 + PARTS - 1)

    far, near = pl.ds(PLACES, SPANS), pl.ds(0, PLACES)
    swap_far = remote(give_ref.at[far], got_ref.at[far], s_core.at[0], r_core.at[0], s, core_peer)
    swap_far.start()
    swap_near = remote(give_ref.at[near], got_ref.at[near], s_core.at[1], r_core.at[1], s, core_peer)
    swap_near.start()

    def part_to(r):
        remote(dmem_ref.at[r], parts_ref.at[r_me], s_part, r_part, part_peer(s, r), u).start()

    others(PARTS, r_me, part_to)
    swap_far.wait_recv()

    def far_to(t):
        out_ref[t] = (keep_ref[PLACES + t].astype(F32) + got_ref[PLACES + t].astype(F32)).astype(BF16)
        remote(out_ref.at[t], back_ref.at[s], s_far, r_far, t, far_place(s, u, t)).start()

    others(SPANS, s, far_to)
    swap_near.wait_recv()

    def add(n):
        total_ref[n] = keep_ref[n].astype(F32) + got_ref[n].astype(F32)

    loop(PLACES, add)
    wait(parts_ref.at[pl.ds(0, PARTS - 1)], r_part)
    parts_ref[r_me] = dmem_ref[r_me]
    part_ref[...] = jnp.sum(parts_ref[...], axis=0)
    wait(back_ref.at[pl.ds(0, SPANS - 1)], r_far)
    wait(out_ref.at[pl.ds(0, SPANS - 1)], s_far)
    wait(parts_ref.at[pl.ds(0, PARTS - 1)], s_part)
    swap_far.wait_send()
    swap_near.wait_send()


def give_back_call(keep, give, dmem):
    tile = (BLOCK, FEATURES)
    return pl.pallas_call(
        give_back,
        in_specs=vmem(3),
        out_specs=vmem(3),
        out_shape=[shape(PLACES, *tile, dtype=F32), shape(SPANS, *tile), shape(ROWS, FEATURES, dtype=F32)],
        scratch_shapes=[
            pltpu.VMEM((PLACES + SPANS,) + tile, BF16),
            pltpu.VMEM((SPANS,) + tile, BF16),
            pltpu.VMEM((PARTS, ROWS, FEATURES), F32),
            DMA((2,)), DMA((2,)), DMA, DMA, DMA, DMA,
        ],
        compiler_params=pltpu.CompilerParams(collective_id=1, has_side_effects=True),
        name="give_back",
    )(keep, give, dmem)


def settle(meta_ref, send_ref, total_ref, back_ref, here_ref, away_ref, acc_ref):
    acc_ref[...] = total_ref[...]
    s, half = meta_ref[1], meta_ref[2]

    @pl.loop(0, SPANS)
    def _(t):
        @pl.when(t != s)
        def _():
            acc_ref[send_ref[t]] += back_ref[t].astype(F32)

    @pl.loop(0, HALF)
    def _(n):
        here_ref[n] = acc_ref[half * HALF + n]
        away_ref[n] = acc_ref[(1 - half) * HALF + n].astype(BF16)


def settle_call(meta, sends, total, back):
    tile = (BLOCK, FEATURES)
    return pl.pallas_call(
        settle,
        in_specs=[SMEM, SMEM] + vmem(2),
        out_specs=vmem(2),
        out_shape=[shape(HALF, *tile, dtype=F32), shape(HALF, *tile)],
        scratch_shapes=[pltpu.VMEM((PLACES,) + tile, F32)],
        name="settle",
    )(meta, sends, total, back)


CHUNKS = 4
RINGS = 6


def deliver(
    gq_ref, here_ref, away_ref, part_ref, gq_out, dk_ref, dv_ref, mem_out,
    got_ref, out_ref, rows_ref, parts_ref, sum_ref,
    s_z, r_z, s_q, r_q, s_rows, r_rows, s_part, r_part, s_mem, r_mem,
):
    s, u, half, p_me, core = position()
    first = half * HALF
    r_me = my_part(s)
    ring_me = (s // X) // 2 * 2 + half
    y = p_me // 2
    head = 4 * y + 2 * core + r_me // 4
    source = first + u // 2

    def ring_peer(r):
        return ((r // 2) * 2 + s // X % 2) * X + s % X, r % 2 * HALF + p_me

    gives = half == y // 4

    def takers(body):
        def step(r):
            blk = part_peer(s, r)

            @pl.when(jnp.logical_not((blk == s) & (head == u)))
            def _():
                body(r, blk)

        loop(PARTS, step)

    def givers(body):
        def step(n):
            blk = part_peer(s, u % 2 * 4 + n)

            @pl.when(jnp.logical_not((blk == s) & (source == u)))
            def _():
                body(blk)

        loop(4, step)

    others(PLACES, u, lambda p: greet(s, p))
    others(RINGS, ring_me, lambda r: greet(*ring_peer(r)))

    @pl.when(gives)
    def _():
        takers(lambda r, blk: greet(blk, head))

    givers(lambda blk: greet(blk, source))
    own = ((r_me // 4 == u % 2) & (source == u)).astype(jnp.int32)
    count = PLACES - 1 + RINGS - 1 + 4 - own + jnp.where(gives, PARTS - own, 0)
    pl.semaphore_wait(pltpu.get_barrier_semaphore(), count)

    each = HALF // CHUNKS
    swaps = []
    for n in range(CHUNKS):
        rows = pl.ds(n * each, each)
        swaps.append(remote(away_ref.at[rows], got_ref.at[rows], s_z.at[n], r_z.at[n], s, (u + HALF) % PLACES))
        swaps[-1].start()

    def part_to(r):
        remote(part_ref, parts_ref.at[ring_me], s_part, r_part, *ring_peer(r)).start()

    others(RINGS, ring_me, part_to)

    def columns(ref, i, width):
        return ref.at[:, pl.ds(pl.multiple_of(i * width, width), width)]

    def gq_to(p):
        send(gq_ref.at[p], columns(gq_out, p_me, 2 * FEATURES), s_q, r_q, s, first + p, p == p_me)

    loop(HALF, gq_to)
    wait(parts_ref.at[pl.ds(0, RINGS - 1)], r_part)
    parts_ref[ring_me] = part_ref[...]
    sum_ref[...] = jnp.sum(parts_ref[...], axis=0)

    def mem_to(r):
        blk = part_peer(s, r)
        send(sum_ref, mem_out.at[r_me % 4], s_mem.at[r], r_mem, blk, head, (blk == s) & (head == u))

    @pl.when(gives)
    def _():
        loop(PARTS, mem_to)

    for n in range(CHUNKS):
        swaps[n].wait_recv()

        def rows_to(i):
            p = n * each + i
            out_ref[p] = (here_ref[p] + got_ref[p].astype(F32)).astype(BF16)
            send(out_ref.at[p], rows_ref.at[p_me], s_rows, r_rows, s, first + p, p == p_me)

        loop(each, rows_to)
    wait(rows_ref, r_rows)
    for head_id in range(KEY_HEADS):
        cols = slice(FEATURES * head_id, FEATURES * (head_id + 1))
        dk_ref[:, cols] = rows_ref[2 * head_id].astype(F32)
        dv_ref[:, cols] = rows_ref[2 * head_id + 1].astype(F32)
    wait(mem_out, r_mem)
    wait(gq_out, r_q)
    wait(out_ref.at[pl.ds(0, HALF - 1)], s_rows)
    wait(gq_out.at[:, pl.ds(0, (HALF - 1) * 2 * FEATURES)], s_q)
    wait(parts_ref.at[pl.ds(0, RINGS - 1)], s_part)
    for n in range(CHUNKS):
        swaps[n].wait_send()

    @pl.when(gives)
    def _():
        takers(lambda r, blk: wait(sum_ref, s_mem.at[r]))


def deliver_call(gq, here, away, part):
    tile = (BLOCK, FEATURES)
    return pl.pallas_call(
        deliver,
        in_specs=vmem(4),
        out_specs=vmem(4),
        out_shape=[
            shape(BLOCK, QUERY_HEADS * FEATURES),
            shape(BLOCK, KEY_HEADS * FEATURES, dtype=F32), shape(BLOCK, KEY_HEADS * FEATURES, dtype=F32),
            shape(4, ROWS, FEATURES, dtype=F32),
        ],
        scratch_shapes=[
            pltpu.VMEM((HALF,) + tile, BF16), pltpu.VMEM((HALF,) + tile, BF16), pltpu.VMEM((HALF,) + tile, BF16),
            pltpu.VMEM((RINGS, ROWS, FEATURES), F32), pltpu.VMEM((ROWS, FEATURES), F32),
            DMA((CHUNKS,)), DMA((CHUNKS,)), DMA, DMA, DMA, DMA, DMA, DMA, DMA((PARTS,)), DMA,
        ],
        compiler_params=pltpu.CompilerParams(collective_id=2, has_side_effects=True),
        name="deliver",
    )(gq, here, away, part)


def shards(queries, keys, values, grad_out, row_lse, row_delta, pattern, memory_keys, memory_values):
    span, place = lax.axis_index("blk"), lax.axis_index("uly")
    half, core = place // HALF, place % 2
    flat = pattern.reshape(SPANS, PLACES * RANDOM)
    ids = jnp.arange(SPANS, dtype=jnp.int32)
    from_me = (flat // PLACES == span) & (ids != span)[:, None]
    named = jnp.sum(jnp.where(from_me, flat % PLACES, 0), axis=1)
    edge = jnp.where(ids > span, PLACES - 1, 0)
    sends = jnp.where(jnp.abs(ids - span) == 1, edge, named)
    mine = lax.dynamic_slice(pattern, (span * PLACES + half * HALF, 0), (HALF, RANDOM))
    mine = jnp.where(mine // PLACES == span, mine % PLACES, PLACES + mine // PLACES)
    b = half * HALF + jnp.arange(HALF, dtype=jnp.int32)
    left_ok = (b > 0) | (span > 0)
    right_ok = (b < PLACES - 1) | (span < SPANS - 1)
    left = jnp.where(b > 0, b - 1, jnp.where(left_ok, PLACES + span - 1, b))
    right = jnp.where(b < PLACES - 1, b + 1, jnp.where(right_ok, PLACES + span + 1, b))
    ends = jnp.stack([left_ok, right_ok], axis=1).astype(jnp.int32)
    index = jnp.concatenate([jnp.stack([left, b, right], axis=1), mine, ends], axis=1)
    meta = jnp.stack([core, span, half]).astype(jnp.int32)

    stats = jnp.stack([row_lse.reshape(2, HALF, BLOCK), row_delta.reshape(2, HALF, BLOCK)], axis=1)
    memory = jnp.stack([memory_keys, memory_values])
    q, do, own, other, far, far_other, stats, memory = gather_call(
        sends, queries, grad_out, keys, values, stats, memory
    )
    gq, keep, give, dmem = attend_call(meta, index, q, do, stats, own, other, far, far_other, memory)
    total, back, part = give_back_call(keep, give, dmem.reshape(PARTS, ROWS, FEATURES))
    here, away = settle_call(meta, sends, total, back)
    gq, dk, dv, mem = deliver_call(gq, here, away, part)
    mem = mem.reshape(2, BLOCK, FEATURES)
    return gq, dk, dv, mem[0], mem[1]


def solution(mesh):
    tokens = P(("blk", "uly"), None)
    heads = P(None, "uly")
    return jax.shard_map(
        shards,
        mesh=mesh,
        in_specs=(tokens, tokens, tokens, tokens, P("blk", "uly"), P("blk", "uly"), P(), heads, heads),
        out_specs=(tokens, tokens, tokens, heads, heads),
        check_vma=False,
    )
```

time: 996 us -> 251 us (0.25)
  the two profiles are of different devices: /device:TPU:8 before, /device:TPU:55 now
where the time goes in v1:
time: 251 us
  Pallas kernels  237 us (94%)
  local copies, waits for them, and re-layouts  7.51 us (3%)
  other arithmetic  4.89 us (2%)
    pallas_call x1, Pallas kernels, gather_call(): pl.pallas_call(gather, in_specs=[SMEM] + hbm(6), out_specs=vmem(8), out_s...  99.7 us
    pallas_call x1, Pallas kernels, deliver_call(): pl.pallas_call(deliver, in_specs=vmem(4), out_specs=vmem(4), out_shape=[s...  78.3 us
    pallas_call x1, Pallas kernels, give_back_call(): pl.pallas_call(give_back, in_specs=vmem(3), out_specs=vmem(3), out_shape=...  32.2 us
    pallas_call x1, Pallas kernels, attend_call(): pl.pallas_call(attend, grid_spec=pltpu.PrefetchScalarGridSpec(num_scalar_...  23.6 us

profile of v1, /device:TPU:55, one launch (start us, length us, event | category | flops | bytes accessed | tf_op | source)
XLA Modules:
  0.0 250.6 jit_solution(15434077619840413492)
XLA Ops:
  0.7 0.6 pad_add_fusion.meta_ref
  1.3 0.7 constant_dynamic-slice_fusion
  2.0 0.1 and.53
  2.1 0.1 and.54
  2.2 0.7 fusion.6
  3.0 0.1 copy.20
  3.1 0.1 copy.21
  3.2 0.1 copy.22
  3.2 0.1 copy.23
  3.4 0.1 reduce_sum.14
  3.4 0.1 reduce_sum.18
  3.5 0.6 compare_select_fusion.1.send_ref
  4.2 0.7 concatenate.3.idx_ref
  4.8 1.4 pad_maximum_fusion.1.stat_ref
  6.2 1.4 pad_maximum_fusion.mem_ref
  7.6 99.7 %gather.1 = (bf16[16,128,256]{2,1,0:T(8,128)(2,1)}, bf16[16,128,256]{2,1,0:T(8,128)(2,1)}, bf16[32,128,128]{2,1,0:T(8,128)(2,1)}, bf16[32,128,128]{2,1,0:T(8,128...) custom-call(s32[24]{0:T(128)} %compare_select_fusion.1.send_ref, ...), custom_call_target="tpu_custom_call" | custom-call | tf_op jit(solution)/shard_map/gather/pallas_call | solution.py:179
  107.3 23.6 %attend.1 = (bf16[16,128,256]{2,1,0:T(8,128)(2,1)}, bf16[56,128,128]{2,1,0:T(8,128)(2,1)}, bf16[56,128,128]{2,1,0:T(8,128)(2,1)}, f32[2,2,128,128]{3,2,1,0:T(8,128)}) custom-call(s32[3]{0:T(128)} %pad_add_fusion.meta_ref, s32[16,7]{1,0:T(8,128)} %concatenate.3.idx_ref, bf16[16,128,256]{2,1,0:T(8,128)(2,1)} %get-tuple-element.26.q_ref, ...), custom_call_target="tpu_custom_call" | custom-call | tf_op jit(solution)/shard_map/attend/pallas_call | solution.py:282
  130.9 32.2 %give_back.1 = (f32[32,128,128]{2,1,0:T(8,128)}, bf16[24,128,128]{2,1,0:T(8,128)(2,1)}, f32[64,128]{1,0:T(8,128)}) custom-call(bf16[56,128,128]{2,1,0:T(8,128)(2,1)} %get-tuple-element.35.keep_ref, bf16[56,128,128]{2,1,0:T(8,128)(2,1)} %get-tuple-element.36.give_ref, f32[8,64,128]{2,1,0:T(8,128)} %bitcast.10), custom_call_target="tpu_custom_call" | custom-call | tf_op jit(solution)/shard_map/give_back/pallas_call | solution.py:357
  163.1 3.6 %settle.1 = (f32[16,128,128]{2,1,0:T(8,128)}, bf16[16,128,128]{2,1,0:T(8,128)(2,1)}) custom-call(s32[3]{0:T(128)} %pad_add_fusion.meta_ref, s32[24]{0:T(128)} %compare_select_fusion.1.send_ref, f32[32,128,128]{2,1,0:T(8,128)} %get-tuple-element.38.total_ref, bf16[24,128,128]{2,1,0:T(8,128)(2,1)} %get-tuple-element.39.back_ref), custom_call_target="tpu_custom_call" | custom-call | tf_op jit(solution)/shard_map/settle/pallas_call | solution.py:391
  166.8 78.3 %deliver.1 = (bf16[128,4096]{1,0:T(8,128)(2,1)}, f32[128,1024]{1,0:T(8,128)}, f32[128,1024]{1,0:T(8,128)}, f32[4,64,128]{2,1,0:T(8,128)}) custom-call(bf16[16,128,256]{2,1,0:T(8,128)(2,1)} %get-tuple-element.34.gq_ref, f32[16,128,128]{2,1,0:T(8,128)} %get-tuple-element.40.here_ref, bf16[16,128,128]{2,1,0:T(8,128)(2,1)} %get-tuple-element.41.away_ref, ...), custom_call_target="tpu_custom_call" | custom-call | tf_op jit(solution)/shard_map/deliver/pallas_call | solution.py:515
  245.1 1.6 fusion.7
  246.7 2.3 copy.27
  249.0 0.8 copy.28
  249.8 0.8 copy.29
  (10 shorter events, 0.1 us)
Async XLA Ops:
  245.1 3.9 %copy-start.1 = (f32[128,1024]{1,0:T(8,128)S(1)}, f32[128,1024]{1,0:T(8,128)}, u32[]{:S(2)}) copy-start(f32[128,1024]{1,0:T(8,128)} %get-tuple-element.59) | copy-start | bytes 1572868
  245.1 4.7 %copy-start = (f32[128,1024]{1,0:T(8,128)S(1)}, f32[128,1024]{1,0:T(8,128)}, u32[]{:S(2)}) copy-start(f32[128,1024]{1,0:T(8,128)} %get-tuple-element.60) | copy-start | bytes 1572868

commit v2 on v1

v2 whole, which is shorter than its diff:
```python
import functools

import jax
import jax.numpy as jnp
from jax import lax
from jax.experimental import pallas as pl
from jax.experimental.pallas import tpu as pltpu
from jax.sharding import PartitionSpec as P

QUERY_HEADS = 32
KEY_HEADS = 8
FEATURES = 128
BLOCK = 128
RANDOM = 2
SLOTS = 3 + RANDOM
SCALE = FEATURES ** (-0.5)
MESH = pl.DeviceIdType.MESH

SPANS, PLACES = 24, 32
HALF = PLACES // 2
YS = HALF // 2
X, Z = 4, 6
PARTS = 8
ROWS = 4 * BLOCK // PARTS

F32, BF16 = jnp.float32, jnp.bfloat16


def position():
    s, u = lax.axis_index("blk"), lax.axis_index("uly")
    return s, u, u // HALF, u % HALF, u % 2


def far_peers(s, u, body):
    x, a = s % X, s // X
    half, p = u // HALF, u % HALF
    odd = x % 2

    def along(step):
        lo = a + step
        crossed = (lo < 0) | (lo >= Z)
        lo = jnp.where(lo < 0, lo + Z, jnp.where(lo >= Z, lo - Z, lo))
        return lo * X, jnp.where(crossed, 1 - half, half) * HALF + p

    for step in (0, 1, -1, 2, -2):
        base, place = along(step)
        for xx in range(X):
            if step:
                body(base + xx, place)
            else:
                pl.when(x != xx)(functools.partial(body, base + xx, place))
    base = jnp.where(a < Z // 2, a + Z // 2, a - Z // 2) * X
    within, across = half * HALF + p, (1 - half) * HALF + p
    even_place = jnp.where(odd == 0, within, across)
    odd_place = jnp.where(odd == 0, across, within)
    for xx in range(X):
        body(base + xx, odd_place if xx % 2 else even_place)


def remote(src, dst, sent, got, blk, uly):
    return pltpu.make_async_remote_copy(
        src_ref=src, dst_ref=dst, send_sem=sent, recv_sem=got, device_id=(blk, uly), device_id_type=MESH
    )


def send(src, dst, sent, got, blk, uly, here):
    @pl.when(jnp.logical_not(here))
    def _():
        remote(src, dst, sent, got, blk, uly).start()

    @pl.when(here)
    def _():
        pltpu.make_async_copy(src, dst, got).start()


def wait(ref, sem):
    pltpu.make_async_copy(ref, ref, sem).wait()


def loop(n, body):
    def step(i, carry):
        body(i)
        return carry

    lax.fori_loop(0, n, step, 0)


def greet(blk, uly):
    pl.semaphore_signal(pltpu.get_barrier_semaphore(), inc=1, device_id=(blk, uly), device_id_type=MESH)


def others(n, me, body):
    def step(i):
        @pl.when(i != me)
        def _():
            body(i)

    loop(n, step)


def part_peer(s, r):
    return ((s // X) // 2 * 2 + r % 2) * X + r // 2


def my_part(s):
    return s % X * 2 + s // X % 2


ENTRIES = HALF * RANDOM
NEAR = HALF + 2
ZERO = ENTRIES + NEAR
CHUNK = 8
MIDDLE = 8


def attend(
    send_ref, entry_ref, named_ref, q_ref, do_ref, k_ref, v_ref, lse_ref, delta_ref, mk_ref, mv_ref,
    gq_ref, sum_ref, back_ref, part_ref,
    qh_ref, doh_ref, own_ref, far_ref, out_ref, pool_ref, terms_ref, got_ref, dq_ref, near_ref, macc_ref,
    stat_ref, mem_ref, dmem_ref, parts_ref,
    s_kv, r_kv, s_q, r_q, s_do, r_do, s_z, r_z, s_core, r_core, c_own, s_far, r_far, s_back, r_back,
    s_stat, r_stat, s_mem, r_mem, s_term, r_term, s_part, r_part,
):
    s, u, half, p_me, core = position()
    y, first = p_me // 2, half * HALF
    second = HALF - first
    core_peer = u + 1 - 2 * core
    r_me = my_part(s)
    others(PLACES, u, lambda p: greet(s, p))
    far_peers(s, u, greet)
    others(PARTS, r_me, lambda r: greet(part_peer(s, r), u))
    pl.semaphore_wait(pltpu.get_barrier_semaphore(), PLACES - 1 + SPANS - 1 + PARTS - 1)

    def columns(ref, i, width):
        return ref.at[:, pl.ds(pl.multiple_of(i * width, width), width)]

    def nearest(n):
        k = (n + 1) // 2
        return (y + jnp.where(n % 2 == 1, k, YS - k)) % YS

    def kv_to(n):
        to = nearest(n)
        for kind, ref in ((0, k_ref), (1, v_ref)):
            place = first + 2 * to + kind
            send(columns(ref, to, FEATURES), own_ref.at[first + p_me], s_kv, r_kv.at[y], s, place, place == u)

    loop(YS, kv_to)
    for z in range(2):
        place = z * HALF + u // 2
        for kind, stat, mem in ((0, lse_ref, mk_ref), (1, delta_ref, mv_ref)):
            send(stat.at[z], stat_ref.at[u % 2, kind], s_stat.at[z, kind], r_stat, s, place, place == u)
            send(mem, mem_ref.at[u % 2, kind], s_mem.at[z, kind], r_mem, s, place, place == u)

    def q_to(n):
        p = 2 * nearest(n // 2) + n % 2
        here = p == p_me
        send(columns(q_ref, p, 2 * FEATURES), qh_ref.at[p_me], s_q, r_q.at[p_me], s, first + p, here)
        send(columns(do_ref, p, 2 * FEATURES), doh_ref.at[p_me], s_do, r_do.at[p_me], s, first + p, here)

    loop(HALF, q_to)
    near_ref[...] = jnp.zeros_like(near_ref)
    macc_ref[...] = jnp.zeros_like(macc_ref)
    for kind in range(2):
        terms_ref[kind, ZERO] = jnp.zeros((BLOCK, FEATURES), BF16)
    got_ref[ZERO] = jnp.zeros((BLOCK, FEATURES), BF16)

    def kv_on(n):
        at = pl.ds(first + 2 * nearest(n), 2)
        piece = own_ref.at[at]
        wait(piece, r_kv.at[nearest(n)])
        remote(piece, piece, s_z, r_z, s, (u + HALF) % PLACES).start()
        remote(piece, pool_ref.at[core, at], s_core.at[0], r_core.at[0], s, core_peer).start()
        pltpu.make_async_copy(piece, pool_ref.at[core, at], c_own.at[0]).start()

    loop(YS, kv_on)
    mine, theirs = pl.ds(first, HALF), pl.ds(second, HALF)
    wait(pool_ref.at[core, mine], c_own.at[0])
    wait(pool_ref.at[1 - core, mine], r_core.at[0])
    wait(stat_ref, r_stat)
    wait(mem_ref, r_mem)

    def dot(a, b, i, j):
        return lax.dot_general(a, b, (((i,), (j,)), ((), ())), preferred_element_type=F32)

    def block(j):
        q = [qh_ref[j, :, FEATURES * i : FEATURES * (i + 1)] for i in range(2)]
        do = [doh_ref[j, :, FEATURES * i : FEATURES * (i + 1)] for i in range(2)]
        lse, delta = [
            jnp.concatenate([stat_ref[i, kind, pl.ds(j, 1), :] for i in range(2)], axis=1) for kind in range(2)
        ]
        return q, do, lse, delta

    def pairs(keys, values, q2, do2, lse, delta, okay=None):
        weights = jnp.exp(dot(keys, q2, 1, 1) * SCALE - lse)
        dscores = weights * (dot(values, do2, 1, 1) - delta)
        if okay is not None:
            weights, dscores = jnp.where(okay, weights, 0.0), jnp.where(okay, dscores, 0.0)
        weight_bf, dscore_bf = weights.astype(BF16), dscores.astype(BF16)
        return dot(dscore_bf, q2, 1, 0) * SCALE, dot(weight_bf, do2, 1, 0), dot(dscore_bf, keys, 0, 0)

    def at_once(j):
        wait(qh_ref.at[j], r_q.at[j])
        wait(doh_ref.at[j], r_do.at[j])
        q, do, lse, delta = block(j)
        for i in range(2):
            cols = slice(FEATURES * i, FEATURES * (i + 1))
            dk, dv, dq = pairs(mem_ref[i, 0], mem_ref[i, 1], q[i], do[i], lse[:, cols], delta[:, cols])
            macc_ref[i, 0] += dk
            macc_ref[i, 1] += dv
            dq_ref[j, BLOCK * i : BLOCK * (i + 1)] = dq

        @pl.when((j > 0) & (j < HALF - 1))
        def _():
            at = pl.ds(first + j - 1, 3)
            keys = pool_ref[0, at].reshape(3 * BLOCK, FEATURES)
            values = pool_ref[1, at].reshape(3 * BLOCK, FEATURES)
            q2, do2 = jnp.concatenate(q, axis=0), jnp.concatenate(do, axis=0)
            dk, dv, dq = pairs(keys, values, q2, do2, lse, delta)
            near_ref[0, pl.ds(j, 3)] += dk.reshape(3, BLOCK, FEATURES)
            near_ref[1, pl.ds(j, 3)] += dv.reshape(3, BLOCK, FEATURES)
            dq_ref[j] += dq

    def in_order(n):
        at_once(2 * nearest(n // 2) + n % 2)

    loop(MIDDLE, in_order)
    wait(own_ref.at[theirs], r_z)
    onward = remote(own_ref.at[theirs], pool_ref.at[core, theirs], s_core.at[1], r_core.at[1], s, core_peer)
    onward.start()
    pltpu.make_async_copy(own_ref.at[theirs], pool_ref.at[core, theirs], c_own.at[1]).start()

    def far_to(t, place):
        out_ref[t] = own_ref[send_ref[t]]
        remote(out_ref.at[t], far_ref.at[s], s_far, r_far, t, place).start()

    far_peers(s, u, far_to)
    loop(HALF - MIDDLE, lambda n: in_order(n + MIDDLE))

    for i in range(2):
        for kind in range(2):
            for n in range(BLOCK // ROWS):
                dmem_ref[i * 4 + kind * 2 + n] = macc_ref[i, kind, ROWS * n : ROWS * (n + 1)]

    def part_to(r):
        remote(dmem_ref.at[r], parts_ref.at[r_me], s_part, r_part, part_peer(s, r), u).start()

    others(PARTS, r_me, part_to)
    rest = pl.ds(0, SPANS - 1)
    far_at = pl.ds(PLACES, SPANS)
    wait(far_ref.at[rest], r_far)
    onward_far = remote(far_ref, pool_ref.at[core, far_at], s_core.at[2], r_core.at[2], s, core_peer)
    onward_far.start()
    pltpu.make_async_copy(far_ref, pool_ref.at[core, far_at], c_own.at[2]).start()
    wait(out_ref.at[rest], s_far)
    for n, at in ((1, theirs), (2, far_at)):
        wait(pool_ref.at[core, at], c_own.at[n])
        wait(pool_ref.at[1 - core, at], r_core.at[n])

    left_okay = (half > 0) | (s > 0)
    right_okay = (half == 0) | (s < SPANS - 1)
    left = jnp.where(half > 0, first - 1, jnp.where(s > 0, PLACES + s - 1, first))
    right = jnp.where(half == 0, HALF, jnp.where(s < SPANS - 1, PLACES + s + 1, first + HALF - 1))
    for j, outer, slot, okay in ((0, left, 0, left_okay), (HALF - 1, right, 2, right_okay)):
        q, do, lse, delta = block(j)
        q2, do2 = jnp.concatenate(q, axis=0), jnp.concatenate(do, axis=0)
        for n, where in ((slot, outer), (1, first + j), (2 - slot, first + (1 if slot == 0 else HALF - 2))):
            dk, dv, dq = pairs(
                pool_ref[0, where], pool_ref[1, where], q2, do2, lse, delta, okay if n == slot else None
            )
            near_ref[0, j + n] += dk
            near_ref[1, j + n] += dv
            dq_ref[j] += dq

    def near_to(n):
        for kind in range(2):
            terms_ref[kind, ENTRIES + n] = near_ref[kind, n].astype(BF16)

    loop(NEAR, near_to)
    chunks = ENTRIES // CHUNK

    def terms_to(n, start, count):
        at = pl.ds(start, count)
        return remote(terms_ref.at[1 - core, at], got_ref.at[at], s_term.at[n], r_term.at[n], s, core_peer)

    terms_to(chunks, ENTRIES, NEAR).start()

    def random(j):
        q, do, lse, delta = block(j)
        which = []
        for r in range(RANDOM):
            named = named_ref[j, r]
            which.append(jnp.where(named // PLACES == s, named % PLACES, PLACES + named // PLACES))
        keys = jnp.concatenate([pool_ref[0, w] for w in which], axis=0)
        values = jnp.concatenate([pool_ref[1, w] for w in which], axis=0)
        dk, dv, dq = pairs(
            keys, values, jnp.concatenate(q, axis=0), jnp.concatenate(do, axis=0), lse, delta
        )
        at = pl.ds(RANDOM * j, RANDOM)
        terms_ref[0, at] = dk.astype(BF16).reshape(RANDOM, BLOCK, FEATURES)
        terms_ref[1, at] = dv.astype(BF16).reshape(RANDOM, BLOCK, FEATURES)
        dq = (dq_ref[j] + dq) * SCALE
        for i in range(2):
            gq_ref[j, :, FEATURES * i : FEATURES * (i + 1)] = dq[BLOCK * i : BLOCK * (i + 1)].astype(BF16)
        per = CHUNK // RANDOM

        @pl.when(j % per == per - 1)
        def _():
            terms_to(j // per, j // per * CHUNK, CHUNK).start()

    loop(HALF, random)
    for n in range(chunks):
        terms_to(n, n * CHUNK, CHUNK).wait()
    terms_to(chunks, ENTRIES, NEAR).wait()

    def back_to(t, place):
        e = entry_ref[t]
        out_ref[t] = (terms_ref[core, e].astype(F32) + got_ref[e].astype(F32)).astype(BF16)
        remote(out_ref.at[t], back_ref.at[s], s_back, r_back, t, place).start()

    far_peers(s, u, back_to)

    def add(n):
        sum_ref[n] = (terms_ref[core, n].astype(F32) + got_ref[n].astype(F32)).astype(BF16)

    loop(ZERO, add)
    wait(parts_ref.at[pl.ds(0, PARTS - 1)], r_part)
    parts_ref[r_me] = dmem_ref[r_me]
    part_ref[...] = jnp.sum(parts_ref[...], axis=0)
    wait(back_ref.at[rest], r_back)
    wait(out_ref.at[rest], s_back)
    wait(parts_ref.at[pl.ds(0, PARTS - 1)], s_part)
    wait(own_ref.at[pl.ds(0, HALF - 1)], s_kv)
    wait(own_ref.at[mine], s_z)
    wait(own_ref.at[mine], s_core.at[0])
    onward.wait_send()
    onward_far.wait_send()
    wait(qh_ref.at[pl.ds(0, HALF - 1)], s_q)
    wait(doh_ref.at[pl.ds(0, HALF - 1)], s_do)
    for z in range(2):
        @pl.when(z * HALF + u // 2 != u)
        def _():
            for kind in range(2):
                wait(stat_ref.at[0, kind], s_stat.at[z, kind])
                wait(mem_ref.at[0, kind], s_mem.at[z, kind])


def vmem(n):
    return [pl.BlockSpec(memory_space=pltpu.VMEM)] * n


def hbm(n):
    return [pl.BlockSpec(memory_space=pl.ANY)] * n


SMEM = pl.BlockSpec(memory_space=pltpu.SMEM)
DMA = pltpu.SemaphoreType.DMA


def shape(*dims, dtype=BF16):
    return jax.ShapeDtypeStruct(dims, dtype)


def attend_call(sends, entries, named, q, do, k, v, lse, delta, mk, mv):
    tile = (BLOCK, FEATURES)
    wide = (HALF, BLOCK, 2 * FEATURES)
    one, per_kind = DMA, DMA((2, 2))
    return pl.pallas_call(
        attend,
        in_specs=[SMEM] * 3 + hbm(8),
        out_specs=vmem(4),
        out_shape=[shape(*wide), shape(ZERO, *tile), shape(SPANS, *tile), shape(ROWS, FEATURES, dtype=F32)],
        scratch_shapes=[
            pltpu.VMEM(wide, BF16),
            pltpu.VMEM(wide, BF16),
            pltpu.VMEM((PLACES,) + tile, BF16),
            pltpu.VMEM((SPANS,) + tile, BF16),
            pltpu.VMEM((SPANS,) + tile, BF16),
            pltpu.VMEM((2, PLACES + SPANS) + tile, BF16),
            pltpu.VMEM((2, ZERO + 1) + tile, BF16),
            pltpu.VMEM((ZERO + 1,) + tile, BF16),
            pltpu.VMEM((HALF, 2 * BLOCK, FEATURES), F32),
            pltpu.VMEM((2, NEAR) + tile, F32),
            pltpu.VMEM((2, 2) + tile, F32),
            pltpu.VMEM((2, 2, HALF, BLOCK), F32),
            pltpu.VMEM((2, 2) + tile, BF16),
            pltpu.VMEM((PARTS, ROWS, FEATURES), F32),
            pltpu.VMEM((PARTS, ROWS, FEATURES), F32),
            one, DMA((YS,)), one, DMA((HALF,)), one, DMA((HALF,)), one, one,
            DMA((3,)), DMA((3,)), DMA((3,)), one, one, one, one,
            per_kind, one, per_kind, one, DMA((5,)), DMA((5,)), one, one,
        ],
        compiler_params=pltpu.CompilerParams(collective_id=0, has_side_effects=True),
        name="attend",
    )(sends, entries, named, q, do, k, v, lse, delta, mk, mv)


def settle(meta_ref, send_ref, named_ref, sum_ref, back_ref, here_ref, away_ref, acc_ref):
    acc_ref[...] = jnp.zeros_like(acc_ref)
    s, half = meta_ref[0], meta_ref[1]

    @pl.loop(0, HALF)
    def _(j):
        for r in range(RANDOM):
            named = named_ref[j, r]

            @pl.when(named // PLACES == s)
            def _():
                acc_ref[named % PLACES] += sum_ref[RANDOM * j + r].astype(F32)

    @pl.loop(0, NEAR)
    def _(n):
        at = half * HALF - 1 + n

        @pl.when((at >= 0) & (at < PLACES))
        def _():
            acc_ref[at] += sum_ref[ENTRIES + n].astype(F32)

    @pl.loop(0, SPANS)
    def _(t):
        @pl.when(t != s)
        def _():
            acc_ref[send_ref[t]] += back_ref[t].astype(F32)

    @pl.loop(0, HALF)
    def _(n):
        here_ref[n] = acc_ref[half * HALF + n]
        away_ref[n] = acc_ref[(1 - half) * HALF + n].astype(BF16)


def settle_call(meta, sends, named, total, back):
    tile = (BLOCK, FEATURES)
    return pl.pallas_call(
        settle,
        in_specs=[SMEM] * 3 + vmem(2),
        out_specs=vmem(2),
        out_shape=[shape(HALF, *tile, dtype=F32), shape(HALF, *tile)],
        scratch_shapes=[pltpu.VMEM((PLACES,) + tile, F32)],
        name="settle",
    )(meta, sends, named, total, back)


CHUNKS = 4
RINGS = 6


def deliver(
    gq_ref, here_ref, away_ref, part_ref, gq_out, dk_ref, dv_ref, mk_out, mv_out,
    mem_out, got_ref, out_ref, rows_ref, parts_ref, sum_ref,
    s_z, r_z, s_q, r_q, s_rows, r_rows, s_part, r_part, s_mem, r_mem,
):
    s, u, half, p_me, core = position()
    first = half * HALF
    r_me = my_part(s)
    ring_me = (s // X) // 2 * 2 + half
    y = p_me // 2
    head = 4 * y + 2 * core + r_me // 4
    source = first + u // 2

    def ring_peer(r):
        return ((r // 2) * 2 + s // X % 2) * X + s % X, r % 2 * HALF + p_me

    gives = half == y // 4

    def takers(body):
        def step(r):
            blk = part_peer(s, r)

            @pl.when(jnp.logical_not((blk == s) & (head == u)))
            def _():
                body(r, blk)

        loop(PARTS, step)

    def givers(body):
        def step(n):
            blk = part_peer(s, u % 2 * 4 + n)

            @pl.when(jnp.logical_not((blk == s) & (source == u)))
            def _():
                body(blk)

        loop(4, step)

    others(HALF, p_me, lambda p: greet(s, first + p))
    greet(s, (u + HALF) % PLACES)
    others(RINGS, ring_me, lambda r: greet(*ring_peer(r)))

    @pl.when(gives)
    def _():
        takers(lambda r, blk: greet(blk, head))

    givers(lambda blk: greet(blk, source))
    own = ((r_me // 4 == u % 2) & (source == u)).astype(jnp.int32)
    count = HALF + RINGS - 1 + 4 - own + jnp.where(gives, PARTS - own, 0)
    pl.semaphore_wait(pltpu.get_barrier_semaphore(), count)

    def part_to(r):
        remote(part_ref, parts_ref.at[ring_me], s_part, r_part, *ring_peer(r)).start()

    others(RINGS, ring_me, part_to)
    each = HALF // CHUNKS
    swaps = []
    for n in range(CHUNKS):
        rows = pl.ds(n * each, each)
        swaps.append(remote(away_ref.at[rows], got_ref.at[rows], s_z.at[n], r_z.at[n], s, (u + HALF) % PLACES))
        swaps[-1].start()

    def columns(ref, i, width):
        return ref.at[:, pl.ds(pl.multiple_of(i * width, width), width)]

    def gq_to(p):
        send(gq_ref.at[p], columns(gq_out, p_me, 2 * FEATURES), s_q, r_q, s, first + p, p == p_me)

    loop(HALF, gq_to)
    for n in range(CHUNKS):
        swaps[n].wait_recv()

        def rows_to(i):
            p = n * each + i
            out_ref[p] = (here_ref[p] + got_ref[p].astype(F32)).astype(BF16)
            send(out_ref.at[p], rows_ref.at[p_me], s_rows, r_rows, s, first + p, p == p_me)

        loop(each, rows_to)
        if n == 0:
            wait(parts_ref.at[pl.ds(0, RINGS - 1)], r_part)
            parts_ref[ring_me] = part_ref[...]
            sum_ref[...] = jnp.sum(parts_ref[...], axis=0)

            def mem_to(r):
                blk = part_peer(s, r)
                send(sum_ref, mem_out.at[r_me % 4], s_mem.at[r], r_mem, blk, head, (blk == s) & (head == u))

            @pl.when(gives)
            def _():
                loop(PARTS, mem_to)
    wait(rows_ref, r_rows)
    for head_id in range(KEY_HEADS):
        cols = slice(FEATURES * head_id, FEATURES * (head_id + 1))
        dk_ref[:, cols] = rows_ref[2 * head_id].astype(F32)
        dv_ref[:, cols] = rows_ref[2 * head_id + 1].astype(F32)
    wait(mem_out, r_mem)
    for n in range(2):
        mk_out[ROWS * n : ROWS * (n + 1), :] = mem_out[n]
        mv_out[ROWS * n : ROWS * (n + 1), :] = mem_out[2 + n]
    wait(gq_out, r_q)
    wait(out_ref.at[pl.ds(0, HALF - 1)], s_rows)
    wait(gq_out.at[:, pl.ds(0, (HALF - 1) * 2 * FEATURES)], s_q)
    wait(parts_ref.at[pl.ds(0, RINGS - 1)], s_part)
    for n in range(CHUNKS):
        swaps[n].wait_send()

    @pl.when(gives)
    def _():
        takers(lambda r, blk: wait(sum_ref, s_mem.at[r]))


def deliver_call(gq, here, away, part):
    tile = (BLOCK, FEATURES)
    return pl.pallas_call(
        deliver,
        in_specs=hbm(1) + vmem(3),
        out_specs=hbm(1) + vmem(4),
        out_shape=[
            shape(BLOCK, QUERY_HEADS * FEATURES),
            shape(BLOCK, KEY_HEADS * FEATURES, dtype=F32), shape(BLOCK, KEY_HEADS * FEATURES, dtype=F32),
            shape(BLOCK, FEATURES, dtype=F32), shape(BLOCK, FEATURES, dtype=F32),
        ],
        scratch_shapes=[
            pltpu.VMEM((4, ROWS, FEATURES), F32),
            pltpu.VMEM((HALF,) + tile, BF16), pltpu.VMEM((HALF,) + tile, BF16), pltpu.VMEM((HALF,) + tile, BF16),
            pltpu.VMEM((RINGS, ROWS, FEATURES), F32), pltpu.VMEM((ROWS, FEATURES), F32),
            DMA((CHUNKS,)), DMA((CHUNKS,)), DMA, DMA, DMA, DMA, DMA, DMA, DMA((PARTS,)), DMA,
        ],
        compiler_params=pltpu.CompilerParams(collective_id=2, has_side_effects=True),
        name="deliver",
    )(gq, here, away, part)


def shards(queries, keys, values, grad_out, row_lse, row_delta, pattern, memory_keys, memory_values):
    span, place = lax.axis_index("blk"), lax.axis_index("uly")
    half = place // HALF
    flat = pattern.reshape(SPANS, PLACES * RANDOM)
    ids = jnp.arange(SPANS, dtype=jnp.int32)
    from_me = (flat // PLACES == span) & (ids != span)[:, None]
    read = jnp.sum(jnp.where(from_me, flat % PLACES, 0), axis=1)
    sends = jnp.where(jnp.abs(ids - span) == 1, jnp.where(ids > span, PLACES - 1, 0), read)
    named = lax.dynamic_slice(pattern, (span * PLACES + half * HALF, 0), (HALF, RANDOM))
    number = jnp.arange(ENTRIES, dtype=jnp.int32).reshape(1, HALF, RANDOM)
    names = (named // PLACES)[None] == ids[:, None, None]
    entries = ZERO + jnp.sum(jnp.where(names, number - ZERO, 0), axis=(1, 2))
    entries = jnp.where((ids == span - 1) & (half == 0), ENTRIES, entries)
    entries = jnp.where((ids == span + 1) & (half == 1), ENTRIES + NEAR - 1, entries)
    meta = jnp.stack([span, half]).astype(jnp.int32)

    rows = (2, HALF, BLOCK)
    gq, total, back, part = attend_call(
        sends, entries, named, queries, grad_out, keys, values,
        row_lse.reshape(rows), row_delta.reshape(rows), memory_keys, memory_values,
    )
    here, away = settle_call(meta, sends, named, total, back)
    return tuple(deliver_call(gq, here, away, part))


def solution(mesh):
    tokens = P(("blk", "uly"), None)
    heads = P(None, "uly")
    return jax.shard_map(
        shards,
        mesh=mesh,
        in_specs=(tokens, tokens, tokens, tokens, P("blk", "uly"), P("blk", "uly"), P(), heads, heads),
        out_specs=(tokens, tokens, tokens, heads, heads),
        check_vma=False,
    )
```

time: 251 us -> 201 us (0.80)
  the two profiles are of different devices: /device:TPU:55 before, /device:TPU:113 now
where the time goes in v2:
time: 201 us
  Pallas kernels  192 us (96%)
  local copies, waits for them, and re-layouts  6.39 us (3%)
  other arithmetic  2.1 us (1%)
    pallas_call x1, Pallas kernels, attend_call(): pl.pallas_call(attend, in_specs=[SMEM] * 3 + hbm(8), out_specs=vmem(4), o...  118 us
    pallas_call x1, Pallas kernels, deliver_call(): pl.pallas_call(deliver, in_specs=hbm(1) + vmem(3), out_specs=hbm(1) + vme...  69.2 us
    unnamed x16, local copies, waits for them, and re-layouts  5.32 us
    pallas_call x1, Pallas kernels, settle_call(): pl.pallas_call(settle, in_specs=[SMEM] * 3 + vmem(2), out_specs=vmem(2),...  4.51 us

profile of v2, /device:TPU:113, one launch (start us, length us, event | category | flops | bytes accessed | tf_op | source)
XLA Modules:
  0.0 201.0 jit_solution(16986097974656196031)
XLA Ops:
  0.7 0.6 pad_add_fusion.meta_ref
  1.3 0.7 constant_dynamic-slice_fusion
  2.0 0.1 and.50
  2.1 0.1 and.51
  2.2 0.7 fusion.2
  2.9 0.1 copy.17.named_ref
  3.0 0.1 copy.16
  3.1 0.1 select_reduce_fusion
  3.2 0.1 reduce_sum.26
  3.3 0.1 reduce_sum.27
  3.4 0.5 and_select_fusion.4
  3.9 0.0 copy-done.2
  3.9 118.1 %attend.1 = (bf16[16,128,256]{2,1,0:T(8,128)(2,1)}, bf16[50,128,128]{2,1,0:T(8,128)(2,1)}, bf16[24,128,128]{2,1,0:T(8,128)(2,1)}, f32[64,128]{1,0:T(8,128)}) custom-call(s32[24]{0:T(128)} %get-tuple-element.18.send_ref, s32[24]{0:T(128)} %get-tuple-element.17.entry_ref, s32[16,2]{1,0:T(8,128)} %copy-done.2, bf16[128,4096]{1,0:T(8,128)(2,1)} %q_ref.1, ...), custom_call_target="tpu_custom_call" | custom-call | tf_op jit(solution)/shard_map/attend/pallas_call | solution.py:367
  122.1 4.5 %settle.1 = (f32[16,128,128]{2,1,0:T(8,128)}, bf16[16,128,128]{2,1,0:T(8,128)(2,1)}) custom-call(s32[2]{0:T(128)} %pad_add_fusion.meta_ref, s32[24]{0:T(128)} %get-tuple-element.18.send_ref, s32[16,2]{1,0:T(8,128)} %copy-done.2, bf16[50,128,128]{2,1,0:T(8,128)(2,1)} %get-tuple-element.12.sum_ref, bf16[24,128,128]{2,1,0:T(8,128)(2,1)} %get-tuple-element.13.back_ref), custom_call_target="tpu_custom_call" | custom-call | tf_op jit(solution)/shard_map/settle/pallas_call | solution.py:432
  126.6 69.2 %deliver.1 = (bf16[128,4096]{1,0:T(8,128)(2,1)}, f32[128,1024]{1,0:T(8,128)}, f32[128,1024]{1,0:T(8,128)}, f32[128,128]{1,0:T(8,128)}, f32[128,128]{1,0:T(8,128)}) custom-call(bf16[16,128,256]{2,1,0:T(8,128)(2,1)} %get-tuple-element.11.gq_ref, f32[16,128,128]{2,1,0:T(8,128)} %get-tuple-element.14.here_ref, bf16[16,128,128]{2,1,0:T(8,128)(2,1)} %get-tuple-element.15.away_ref, ...), custom_call_target="tpu_custom_call" | custom-call | tf_op jit(solution)/shard_map/deliver/pallas_call | solution.py:559
  195.7 0.0 copy-start.1
  195.8 0.0 copy-start
  195.8 0.0 copy-start.4
  195.8 2.4 %copy.23 = bf16[128,4096]{1,0:T(8,128)(2,1)} copy(bf16[128,4096]{1,0:T(8,128)(2,1)} %get-tuple-element.24) | data formatting | bytes 2097152
  198.2 0.8 copy.24
  199.0 0.8 copy.25
  199.7 0.0 copy-done.4
  199.7 0.6 copy.26
  200.4 0.6 copy.27
  (8 shorter events, 0.0 us)
Async XLA Ops:
  3.0 0.9 copy-start.2
  195.7 2.4 %copy-start.1 = (f32[128,1024]{1,0:T(8,128)S(1)}, f32[128,1024]{1,0:T(8,128)}, u32[]{:S(2)}) copy-start(f32[128,1024]{1,0:T(8,128)} %get-tuple-element.25) | copy-start | bytes 1572868
  195.8 3.2 %copy-start = (f32[128,1024]{1,0:T(8,128)S(1)}, f32[128,1024]{1,0:T(8,128)}, u32[]{:S(2)}) copy-start(f32[128,1024]{1,0:T(8,128)} %get-tuple-element.26) | copy-start | bytes 1572868
  195.8 4.0 %copy-start.4 = (f32[128,128]{1,0:T(8,128)S(1)}, f32[128,128]{1,0:T(8,128)}, u32[]{:S(2)}) copy-start(f32[128,128]{1,0:T(8,128)} %get-tuple-element.27) | copy-start | bytes 196612
  198.2 2.2 %copy-start.3 = (f32[128,128]{1,0:T(8,128)S(1)}, f32[128,128]{1,0:T(8,128)}, u32[]{:S(2)}) copy-start(f32[128,128]{1,0:T(8,128)} %get-tuple-element.28) | copy-start | bytes 196612

commit v3 on v2

--- a/solution.py
+++ b/solution.py
@@ -109,27 +109,71 @@
 ENTRIES = HALF * RANDOM
 NEAR = HALF + 2
 ZERO = ENTRIES + NEAR
+LINKS = ENTRIES + SPANS
+CHUNKS = 4
+RINGS = 6
 CHUNK = 8
 MIDDLE = 8
 
 
 def attend(
-    send_ref, entry_ref, named_ref, q_ref, do_ref, k_ref, v_ref, lse_ref, delta_ref, mk_ref, mv_ref,
-    gq_ref, sum_ref, back_ref, part_ref,
+    send_ref, entry_ref, named_ref, before_ref, last_ref,
+    q_ref, do_ref, k_ref, v_ref, lse_ref, delta_ref, mk_ref, mv_ref,
+    gq_out, dk_ref, dv_ref, mk_out, mv_out,
+    gq_ref, chain_ref, back_ref, part_ref, away_ref, came_ref, rows_out, rows_ref, rings_ref, total_ref, mem_out,
     qh_ref, doh_ref, own_ref, far_ref, out_ref, pool_ref, terms_ref, got_ref, dq_ref, near_ref, macc_ref,
     stat_ref, mem_ref, dmem_ref, parts_ref,
     s_kv, r_kv, s_q, r_q, s_do, r_do, s_z, r_z, s_core, r_core, c_own, s_far, r_far, s_back, r_back,
     s_stat, r_stat, s_mem, r_mem, s_term, r_term, s_part, r_part,
+    s_gq, r_gq, s_away, r_away, s_rows, r_rows, s_ring, r_ring, s_out, r_out,
 ):
     s, u, half, p_me, core = position()
     y, first = p_me // 2, half * HALF
     second = HALF - first
     core_peer = u + 1 - 2 * core
     r_me = my_part(s)
+    ring_me = (s // X) // 2 * 2 + half
+    head = 4 * y + 2 * core + r_me // 4
+    source = first + u // 2
+
+    def ring_peer(r):
+        return ((r // 2) * 2 + s // X % 2) * X + s % X, r % 2 * HALF + p_me
+
+    gives = half == y // 4
+
+    def takers(body):
+        def step(r):
+            blk = part_peer(s, r)
+
+            @pl.when(jnp.logical_not((blk == s) & (head == u)))
+            def _():
+                body(r, blk)
+
+        loop(PARTS, step)
+
+    def givers(body):
+        def step(n):
+            blk = part_peer(s, u % 2 * 4 + n)
+
+            @pl.when(jnp.logical_not((blk == s) & (source == u)))
+            def _():
+                body(blk)
+
+        loop(4, step)
+
     others(PLACES, u, lambda p: greet(s, p))
     far_peers(s, u, greet)
     others(PARTS, r_me, lambda r: greet(part_peer(s, r), u))
-    pl.semaphore_wait(pltpu.get_barrier_semaphore(), PLACES - 1 + SPANS - 1 + PARTS - 1)
+    others(RINGS, ring_me, lambda r: greet(*ring_peer(r)))
+
+    @pl.when(gives)
+    def _():
+        takers(lambda r, blk: greet(blk, head))
+
+    givers(lambda blk: greet(blk, source))
+    own = ((r_me // 4 == u % 2) & (source == u)).astype(jnp.int32)
+    count = PLACES - 1 + SPANS - 1 + PARTS - 1 + RINGS - 1 + 4 - own + jnp.where(gives, PARTS - own, 0)
+    pl.semaphore_wait(pltpu.get_barrier_semaphore(), count)
 
     def columns(ref, i, width):
         return ref.at[:, pl.ds(pl.multiple_of(i * width, width), width)]
@@ -163,6 +207,7 @@
     for kind in range(2):
         terms_ref[kind, ZERO] = jnp.zeros((BLOCK, FEATURES), BF16)
     got_ref[ZERO] = jnp.zeros((BLOCK, FEATURES), BF16)
+    chain_ref[LINKS] = jnp.zeros((BLOCK, FEATURES), F32)
 
     def kv_on(n):
         at = pl.ds(first + 2 * nearest(n), 2)
@@ -301,6 +346,7 @@
         dq = (dq_ref[j] + dq) * SCALE
         for i in range(2):
             gq_ref[j, :, FEATURES * i : FEATURES * (i + 1)] = dq[BLOCK * i : BLOCK * (i + 1)].astype(BF16)
+        send(gq_ref.at[j], columns(gq_out, p_me, 2 * FEATURES), s_gq, r_gq, s, first + j, j == p_me)
         per = CHUNK // RANDOM
 
         @pl.when(j % per == per - 1)
@@ -319,14 +365,84 @@
 
     far_peers(s, u, back_to)
 
-    def add(n):
-        sum_ref[n] = (terms_ref[core, n].astype(F32) + got_ref[n].astype(F32)).astype(BF16)
-
-    loop(ZERO, add)
     wait(parts_ref.at[pl.ds(0, PARTS - 1)], r_part)
     parts_ref[r_me] = dmem_ref[r_me]
     part_ref[...] = jnp.sum(parts_ref[...], axis=0)
+
+    def ring_to(r):
+        remote(part_ref, rings_ref.at[ring_me], s_ring, r_ring, *ring_peer(r)).start()
+
+    others(RINGS, ring_me, ring_to)
+
+    def both(n):
+        return terms_ref[core, n].astype(F32) + got_ref[n].astype(F32)
+
+    def link(n):
+        chain_ref[n] = both(n) + chain_ref[before_ref[n]]
+
+    loop(ENTRIES, link)
     wait(back_ref.at[rest], r_back)
+
+    def link_back(t):
+        chain_ref[ENTRIES + t] = back_ref[t].astype(F32) + chain_ref[before_ref[ENTRIES + t]]
+
+    others(SPANS, s, link_back)
+    each = HALF // CHUNKS
+    swaps = []
+    beside, edge = jnp.where(half == 0, 0, HALF - 1), jnp.where(half == 0, NEAR - 1, 0)
+
+    def away(n):
+        met = jnp.where(n == beside, both(ENTRIES + edge), 0.0)
+        away_ref[n] = (chain_ref[last_ref[second + n]] + met).astype(BF16)
+
+    for c in range(CHUNKS):
+        loop(each, lambda i: away(c * each + i))
+        at = pl.ds(c * each, each)
+        swaps.append(remote(away_ref.at[at], came_ref.at[at], s_away.at[c], r_away.at[c], s, (u + HALF) % PLACES))
+        swaps[-1].start()
+
+    wait(rings_ref.at[pl.ds(0, RINGS - 1)], r_ring)
+    rings_ref[ring_me] = part_ref[...]
+    total_ref[...] = jnp.sum(rings_ref[...], axis=0)
+
+    def mem_to(r):
+        blk = part_peer(s, r)
+        send(total_ref, mem_out.at[r_me % 4], s_out.at[r], r_out, blk, head, (blk == s) & (head == u))
+
+    @pl.when(gives)
+    def _():
+        loop(PARTS, mem_to)
+
+    for c in range(CHUNKS):
+        swaps[c].wait_recv()
+
+        def rows_to(i):
+            p = c * each + i
+            here = chain_ref[last_ref[first + p]] + both(ENTRIES + 1 + p)
+            rows_out[p] = (here + came_ref[p].astype(F32)).astype(BF16)
+            send(rows_out.at[p], rows_ref.at[p_me], s_rows, r_rows, s, first + p, p == p_me)
+
+        loop(each, rows_to)
+    wait(mem_out, r_out)
+    for n in range(2):
+        mk_out[ROWS * n : ROWS * (n + 1), :] = mem_out[n]
+        mv_out[ROWS * n : ROWS * (n + 1), :] = mem_out[2 + n]
+    wait(rows_ref, r_rows)
+    for head_id in range(KEY_HEADS):
+        cols = slice(FEATURES * head_id, FEATURES * (head_id + 1))
+        dk_ref[:, cols] = rows_ref[2 * head_id].astype(F32)
+        dv_ref[:, cols] = rows_ref[2 * head_id + 1].astype(F32)
+    wait(gq_out, r_gq)
+    wait(rows_out.at[pl.ds(0, HALF - 1)], s_rows)
+    wait(gq_ref.at[pl.ds(0, HALF - 1)], s_gq)
+    wait(rings_ref.at[pl.ds(0, RINGS - 1)], s_ring)
+    for c in range(CHUNKS):
+        swaps[c].wait_send()
+
+    @pl.when(gives)
+    def _():
+        takers(lambda r, blk: wait(total_ref, s_out.at[r]))
+
     wait(out_ref.at[rest], s_back)
     wait(parts_ref.at[pl.ds(0, PARTS - 1)], s_part)
     wait(own_ref.at[pl.ds(0, HALF - 1)], s_kv)
@@ -360,16 +476,29 @@
     return jax.ShapeDtypeStruct(dims, dtype)
 
 
-def attend_call(sends, entries, named, q, do, k, v, lse, delta, mk, mv):
+def attend_call(sends, entries, named, before, last, q, do, k, v, lse, delta, mk, mv):
     tile = (BLOCK, FEATURES)
     wide = (HALF, BLOCK, 2 * FEATURES)
     one, per_kind = DMA, DMA((2, 2))
     return pl.pallas_call(
         attend,
-        in_specs=[SMEM] * 3 + hbm(8),
-        out_specs=vmem(4),
-        out_shape=[shape(*wide), shape(ZERO, *tile), shape(SPANS, *tile), shape(ROWS, FEATURES, dtype=F32)],
+        in_specs=[SMEM] * 5 + hbm(8),
+        out_specs=hbm(1) + vmem(4),
+        out_shape=[shape(BLOCK, QUERY_HEADS * FEATURES)]
+        + [shape(BLOCK, KEY_HEADS * FEATURES, dtype=F32)] * 2
+        + [shape(BLOCK, FEATURES, dtype=F32)] * 2,
         scratch_shapes=[
+            pltpu.VMEM(wide, BF16),
+            pltpu.VMEM((LINKS + 1,) + tile, F32),
+            pltpu.VMEM((SPANS,) + tile, BF16),
+            pltpu.VMEM((ROWS, FEATURES), F32),
+            pltpu.VMEM((HALF,) + tile, BF16),
+            pltpu.VMEM((HALF,) + tile, BF16),
+            pltpu.VMEM((HALF,) + tile, BF16),
+            pltpu.VMEM((HALF,) + tile, BF16),
+            pltpu.VMEM((RINGS, ROWS, FEATURES), F32),
+            pltpu.VMEM((ROWS, FEATURES), F32),
+            pltpu.VMEM((4, ROWS, FEATURES), F32),
             pltpu.VMEM(wide, BF16),
             pltpu.VMEM(wide, BF16),
             pltpu.VMEM((PLACES,) + tile, BF16),
@@ -388,192 +517,11 @@
             one, DMA((YS,)), one, DMA((HALF,)), one, DMA((HALF,)), one, one,
             DMA((3,)), DMA((3,)), DMA((3,)), one, one, one, one,
             per_kind, one, per_kind, one, DMA((5,)), DMA((5,)), one, one,
+            one, one, DMA((CHUNKS,)), DMA((CHUNKS,)), one, one, one, one, DMA((PARTS,)), one,
         ],
         compiler_params=pltpu.CompilerParams(collective_id=0, has_side_effects=True),
         name="attend",
-    )(sends, entries, named, q, do, k, v, lse, delta, mk, mv)
-
-
-def settle(meta_ref, send_ref, named_ref, sum_ref, back_ref, here_ref, away_ref, acc_ref):
-    acc_ref[...] = jnp.zeros_like(acc_ref)
-    s, half = meta_ref[0], meta_ref[1]
-
-    @pl.loop(0, HALF)
-    def _(j):
-        for r in range(RANDOM):
-            named = named_ref[j, r]
-
-            @pl.when(named // PLACES == s)
-            def _():
-                acc_ref[named % PLACES] += sum_ref[RANDOM * j + r].astype(F32)
-
-    @pl.loop(0, NEAR)
-    def _(n):
-        at = half * HALF - 1 + n
-
-        @pl.when((at >= 0) & (at < PLACES))
-        def _():
-            acc_ref[at] += sum_ref[ENTRIES + n].astype(F32)
-
-    @pl.loop(0, SPANS)
-    def _(t):
-        @pl.when(t != s)
-        def _():
-            acc_ref[send_ref[t]] += back_ref[t].astype(F32)
-
-    @pl.loop(0, HALF)
-    def _(n):
-        here_ref[n] = acc_ref[half * HALF + n]
-        away_ref[n] = acc_ref[(1 - half) * HALF + n].astype(BF16)
-
-
-def settle_call(meta, sends, named, total, back):
-    tile = (BLOCK, FEATURES)
-    return pl.pallas_call(
-        settle,
-        in_specs=[SMEM] * 3 + vmem(2),
-        out_specs=vmem(2),
-        out_shape=[shape(HALF, *tile, dtype=F32), shape(HALF, *tile)],
-        scratch_shapes=[pltpu.VMEM((PLACES,) + tile, F32)],
-        name="settle",
-    )(meta, sends, named, total, back)
-
-
-CHUNKS = 4
-RINGS = 6
-
-
-def deliver(
-    gq_ref, here_ref, away_ref, part_ref, gq_out, dk_ref, dv_ref, mk_out, mv_out,
-    mem_out, got_ref, out_ref, rows_ref, parts_ref, sum_ref,
-    s_z, r_z, s_q, r_q, s_rows, r_rows, s_part, r_part, s_mem, r_mem,
-):
-    s, u, half, p_me, core = position()
-    first = half * HALF
-    r_me = my_part(s)
-    ring_me = (s // X) // 2 * 2 + half
-    y = p_me // 2
-    head = 4 * y + 2 * core + r_me // 4
-    source = first + u // 2
-
-    def ring_peer(r):
-        return ((r // 2) * 2 + s // X % 2) * X + s % X, r % 2 * HALF + p_me
-
-    gives = half == y // 4
-
-    def takers(body):
-        def step(r):
-            blk = part_peer(s, r)
-
-            @pl.when(jnp.logical_not((blk == s) & (head == u)))
-            def _():
-                body(r, blk)
-
-        loop(PARTS, step)
-
-    def givers(body):
-        def step(n):
-            blk = part_peer(s, u % 2 * 4 + n)
-
-            @pl.when(jnp.logical_not((blk == s) & (source == u)))
-            def _():
-                body(blk)
-
-        loop(4, step)
-
-    others(HALF, p_me, lambda p: greet(s, first + p))
-    greet(s, (u + HALF) % PLACES)
-    others(RINGS, ring_me, lambda r: greet(*ring_peer(r)))
-
-    @pl.when(gives)
-    def _():
-        takers(lambda r, blk: greet(blk, head))
-
-    givers(lambda blk: greet(blk, source))
-    own = ((r_me // 4 == u % 2) & (source == u)).astype(jnp.int32)
-    count = HALF + RINGS - 1 + 4 - own + jnp.where(gives, PARTS - own, 0)
-    pl.semaphore_wait(pltpu.get_barrier_semaphore(), count)
-
-    def part_to(r):
-        remote(part_ref, parts_ref.at[ring_me], s_part, r_part, *ring_peer(r)).start()
-
-    others(RINGS, ring_me, part_to)
-    each = HALF // CHUNKS
-    swaps = []
-    for n in range(CHUNKS):
-        rows = pl.ds(n * each, each)
-        swaps.append(remote(away_ref.at[rows], got_ref.at[rows], s_z.at[n], r_z.at[n], s, (u + HALF) % PLACES))
-        swaps[-1].start()
-
-    def columns(ref, i, width):
-        return ref.at[:, pl.ds(pl.multiple_of(i * width, width), width)]
-
-    def gq_to(p):
-        send(gq_ref.at[p], columns(gq_out, p_me, 2 * FEATURES), s_q, r_q, s, first + p, p == p_me)
-
-    loop(HALF, gq_to)
-    for n in range(CHUNKS):
-        swaps[n].wait_recv()
-
-        def rows_to(i):
-            p = n * each + i
-            out_ref[p] = (here_ref[p] + got_ref[p].astype(F32)).astype(BF16)
-            send(out_ref.at[p], rows_ref.at[p_me], s_rows, r_rows, s, first + p, p == p_me)
-
-        loop(each, rows_to)
-        if n == 0:
-            wait(parts_ref.at[pl.ds(0, RINGS - 1)], r_part)
-            parts_ref[ring_me] = part_ref[...]
-            sum_ref[...] = jnp.sum(parts_ref[...], axis=0)
-
-            def mem_to(r):
-                blk = part_peer(s, r)
-                send(sum_ref, mem_out.at[r_me % 4], s_mem.at[r], r_mem, blk, head, (blk == s) & (head == u))
-
-            @pl.when(gives)
-            def _():
-                loop(PARTS, mem_to)
-    wait(rows_ref, r_rows)
-    for head_id in range(KEY_HEADS):
-        cols = slice(FEATURES * head_id, FEATURES * (head_id + 1))
-        dk_ref[:, cols] = rows_ref[2 * head_id].astype(F32)
-        dv_ref[:, cols] = rows_ref[2 * head_id + 1].astype(F32)
-    wait(mem_out, r_mem)
-    for n in range(2):
-        mk_out[ROWS * n : ROWS * (n + 1), :] = mem_out[n]
-        mv_out[ROWS * n : ROWS * (n + 1), :] = mem_out[2 + n]
-    wait(gq_out, r_q)
-    wait(out_ref.at[pl.ds(0, HALF - 1)], s_rows)
-    wait(gq_out.at[:, pl.ds(0, (HALF - 1) * 2 * FEATURES)], s_q)
-    wait(parts_ref.at[pl.ds(0, RINGS - 1)], s_part)
-    for n in range(CHUNKS):
-        swaps[n].wait_send()
-
-    @pl.when(gives)
-    def _():
-        takers(lambda r, blk: wait(sum_ref, s_mem.at[r]))
-
-
-def deliver_call(gq, here, away, part):
-    tile = (BLOCK, FEATURES)
-    return pl.pallas_call(
-        deliver,
-        in_specs=hbm(1) + vmem(3),
-        out_specs=hbm(1) + vmem(4),
-        out_shape=[
-            shape(BLOCK, QUERY_HEADS * FEATURES),
-            shape(BLOCK, KEY_HEADS * FEATURES, dtype=F32), shape(BLOCK, KEY_HEADS * FEATURES, dtype=F32),
-            shape(BLOCK, FEATURES, dtype=F32), shape(BLOCK, FEATURES, dtype=F32),
-        ],
-        scratch_shapes=[
-            pltpu.VMEM((4, ROWS, FEATURES), F32),
-            pltpu.VMEM((HALF,) + tile, BF16), pltpu.VMEM((HALF,) + tile, BF16), pltpu.VMEM((HALF,) + tile, BF16),
-            pltpu.VMEM((RINGS, ROWS, FEATURES), F32), pltpu.VMEM((ROWS, FEATURES), F32),
-            DMA((CHUNKS,)), DMA((CHUNKS,)), DMA, DMA, DMA, DMA, DMA, DMA, DMA((PARTS,)), DMA,
-        ],
-        compiler_params=pltpu.CompilerParams(collective_id=2, has_side_effects=True),
-        name="deliver",
-    )(gq, here, away, part)
+    )(sends, entries, named, before, last, q, do, k, v, lse, delta, mk, mv)
 
 
 def shards(queries, keys, values, grad_out, row_lse, row_delta, pattern, memory_keys, memory_values):
@@ -590,15 +538,22 @@
     entries = ZERO + jnp.sum(jnp.where(names, number - ZERO, 0), axis=(1, 2))
     entries = jnp.where((ids == span - 1) & (half == 0), ENTRIES, entries)
     entries = jnp.where((ids == span + 1) & (half == 1), ENTRIES + NEAR - 1, entries)
-    meta = jnp.stack([span, half]).astype(jnp.int32)
+    links = jnp.arange(LINKS, dtype=jnp.int32)
+    blocks = jnp.concatenate(
+        [jnp.where(named // PLACES == span, named % PLACES, -1).reshape(ENTRIES), jnp.where(ids == span, -1, sends)]
+    )
+    earlier = (blocks[:, None] == blocks[None]) & (links[:, None] > links[None])
+    before = jnp.max(jnp.where(earlier, links[None], -1), axis=1)
+    before = jnp.where(before < 0, LINKS, before)
+    naming = blocks[None] == jnp.arange(PLACES, dtype=jnp.int32)[:, None]
+    last = jnp.max(jnp.where(naming, links[None], -1), axis=1)
+    last = jnp.where(last < 0, LINKS, last)
 
     rows = (2, HALF, BLOCK)
-    gq, total, back, part = attend_call(
-        sends, entries, named, queries, grad_out, keys, values,
+    return tuple(attend_call(
+        sends, entries, named, before, last, queries, grad_out, keys, values,
         row_lse.reshape(rows), row_delta.reshape(rows), memory_keys, memory_values,
-    )
-    here, away = settle_call(meta, sends, named, total, back)
-    return tuple(deliver_call(gq, here, away, part))
+    ))
 
 
 def solution(mesh):

time: 201 us -> 181 us (0.900)
  the two profiles are of different devices: /device:TPU:113 before, /device:TPU:49 now
where the time goes in v3:
time: 181 us
  Pallas kernels  170 us (94%)
  local copies, waits for them, and re-layouts  7.57 us (4%)
  other arithmetic  2.21 us (1%)
    pallas_call x1, Pallas kernels, attend_call(): pl.pallas_call(attend, in_specs=[SMEM] * 5 + hbm(8), out_specs=hbm(1) + v...  170 us
    unnamed x18, local copies, waits for them, and re-layouts  7.11 us

profile of v3, /device:TPU:49, one launch (start us, length us, event | category | flops | bytes accessed | tf_op | source)
XLA Modules:
  0.0 180.7 jit_solution(9716035043210081680)
XLA Ops:
  0.7 0.7 copy-done.5
  1.4 0.1 constant_dynamic-slice_fusion
  1.4 0.1 and.59
  1.5 0.1 and.60
  1.6 0.1 copy.18.named_ref
  1.8 0.1 reduce_sum.27
  1.9 0.4 copy-done.2
  2.3 0.1 reshape.51
  2.4 0.1 copy.17
  2.5 0.1 select_reduce_fusion.2
  2.6 0.5 compare_select_fusion.2
  3.1 0.1 pad_add_fusion
  3.2 0.2 select_reduce_fusion
  3.4 0.1 select_reduce_fusion.1
  3.5 0.5 compare_select_fusion.last_ref
  4.0 0.5 compare_select_fusion.1.before_ref
  4.5 170.2 %attend.1 = (bf16[128,4096]{1,0:T(8,128)(2,1)}, f32[128,1024]{1,0:T(8,128)}, f32[128,1024]{1,0:T(8,128)}, f32[128,128]{1,0:T(8,128)}, f32[128,128]{1,0:T(8,128)}) custom-call(s32[24]{0:T(128)} %get-tuple-element.6.send_ref, s32[24]{0:T(128)} %get-tuple-element.9.entry_ref, s32[16,2]{1,0:T(8,128)} %copy-done.2, s32[56]{0:T(128)} %compare_select_fusion.1.before_ref, ...), custom_call_target="tpu_custom_call" | custom-call | tf_op jit(solution)/shard_map/attend/pallas_call | solution.py:483
  174.8 2.3 %copy.24 = bf16[128,4096]{1,0:T(8,128)(2,1)} copy(bf16[128,4096]{1,0:T(8,128)(2,1)} %get-tuple-element.15) | data formatting | bytes 2097152
  177.1 0.8 copy.25
  177.9 0.4 copy-done
  178.4 0.8 copy.26
  179.2 0.6 copy.27
  179.9 0.2 copy-done.3
  180.1 0.6 copy.28
  (13 shorter events, 0.2 us)
Async XLA Ops:
  0.7 0.7 copy-start.5
  1.7 0.6 copy-start.2
  174.8 2.4 %copy-start.1 = (f32[128,1024]{1,0:T(8,128)S(1)}, f32[128,1024]{1,0:T(8,128)}, u32[]{:S(2)}) copy-start(f32[128,1024]{1,0:T(8,128)} %get-tuple-element.16) | copy-start | bytes 1572868
  177.1 1.2 copy-start
  178.4 0.9 copy-start.4
  179.2 0.9 copy-start.3

commit v4 on v3

--- a/solution.py
+++ b/solution.py
@@ -114,13 +114,14 @@
 RINGS = 6
 CHUNK = 8
 MIDDLE = 8
+LATE = 14
 
 
 def attend(
     send_ref, entry_ref, named_ref, before_ref, last_ref,
     q_ref, do_ref, k_ref, v_ref, lse_ref, delta_ref, mk_ref, mv_ref,
-    gq_out, dk_ref, dv_ref, mk_out, mv_out,
-    gq_ref, chain_ref, back_ref, part_ref, away_ref, came_ref, rows_out, rows_ref, rings_ref, total_ref, mem_out,
+    gq_out, rows_ref, mem_out,
+    gq_ref, chain_ref, back_ref, part_ref, away_ref, came_ref, rows_out, rings_ref, total_ref,
     qh_ref, doh_ref, own_ref, far_ref, out_ref, pool_ref, terms_ref, got_ref, dq_ref, near_ref, macc_ref,
     stat_ref, mem_ref, dmem_ref, parts_ref,
     s_kv, r_kv, s_q, r_q, s_do, r_do, s_z, r_z, s_core, r_core, c_own, s_far, r_far, s_back, r_back,
@@ -254,16 +255,20 @@
             macc_ref[i, 1] += dv
             dq_ref[j, BLOCK * i : BLOCK * (i + 1)] = dq
 
-        @pl.when((j > 0) & (j < HALF - 1))
-        def _():
-            at = pl.ds(first + j - 1, 3)
-            keys = pool_ref[0, at].reshape(3 * BLOCK, FEATURES)
-            values = pool_ref[1, at].reshape(3 * BLOCK, FEATURES)
-            q2, do2 = jnp.concatenate(q, axis=0), jnp.concatenate(do, axis=0)
+        q2, do2 = jnp.concatenate(q, axis=0), jnp.concatenate(do, axis=0)
+
+        def window(start, met, count):
+            at, to = pl.ds(first + start, count), pl.ds(met, count)
+            keys = pool_ref[0, at].reshape(count * BLOCK, FEATURES)
+            values = pool_ref[1, at].reshape(count * BLOCK, FEATURES)
             dk, dv, dq = pairs(keys, values, q2, do2, lse, delta)
-            near_ref[0, pl.ds(j, 3)] += dk.reshape(3, BLOCK, FEATURES)
-            near_ref[1, pl.ds(j, 3)] += dv.reshape(3, BLOCK, FEATURES)
+            near_ref[0, to] += dk.reshape(count, BLOCK, FEATURES)
+            near_ref[1, to] += dv.reshape(count, BLOCK, FEATURES)
             dq_ref[j] += dq
+
+        inside = (j > 0) & (j < HALF - 1)
+        pl.when(inside)(lambda: window(j - 1, j, 3))
+        pl.when(jnp.logical_not(inside))(lambda: window(jnp.where(j == 0, 0, HALF - 2), jnp.where(j == 0, 1, HALF - 1), 2))
 
     def in_order(n):
         at_once(2 * nearest(n // 2) + n % 2)
@@ -276,10 +281,19 @@
 
     def far_to(t, place):
         out_ref[t] = own_ref[send_ref[t]]
-        remote(out_ref.at[t], far_ref.at[s], s_far, r_far, t, place).start()
+        remote(out_ref.at[t], far_ref.at[s], s_far, r_far.at[s], t, place).start()
 
     far_peers(s, u, far_to)
-    loop(HALF - MIDDLE, lambda n: in_order(n + MIDDLE))
+    loop(LATE - MIDDLE, lambda n: in_order(n + MIDDLE))
+
+    def far_on(t, place):
+        wait(far_ref.at[t], r_far.at[t])
+        at = pool_ref.at[core, PLACES + t]
+        remote(far_ref.at[t], at, s_core.at[2], r_core.at[2], s, core_peer).start()
+        pltpu.make_async_copy(far_ref.at[t], at, c_own.at[2]).start()
+
+    far_peers(s, u, far_on)
+    loop(HALF - LATE, lambda n: in_order(n + LATE))
 
     for i in range(2):
         for kind in range(2):
@@ -291,11 +305,7 @@
 
     others(PARTS, r_me, part_to)
     rest = pl.ds(0, SPANS - 1)
-    far_at = pl.ds(PLACES, SPANS)
-    wait(far_ref.at[rest], r_far)
-    onward_far = remote(far_ref, pool_ref.at[core, far_at], s_core.at[2], r_core.at[2], s, core_peer)
-    onward_far.start()
-    pltpu.make_async_copy(far_ref, pool_ref.at[core, far_at], c_own.at[2]).start()
+    far_at = pl.ds(PLACES, SPANS - 1)
     wait(out_ref.at[rest], s_far)
     for n, at in ((1, theirs), (2, far_at)):
         wait(pool_ref.at[core, at], c_own.at[n])
@@ -305,16 +315,15 @@
     right_okay = (half == 0) | (s < SPANS - 1)
     left = jnp.where(half > 0, first - 1, jnp.where(s > 0, PLACES + s - 1, first))
     right = jnp.where(half == 0, HALF, jnp.where(s < SPANS - 1, PLACES + s + 1, first + HALF - 1))
-    for j, outer, slot, okay in ((0, left, 0, left_okay), (HALF - 1, right, 2, right_okay)):
+    made = []
+    for j, outer, okay in ((0, left, left_okay), (HALF - 1, right, right_okay)):
         q, do, lse, delta = block(j)
         q2, do2 = jnp.concatenate(q, axis=0), jnp.concatenate(do, axis=0)
-        for n, where in ((slot, outer), (1, first + j), (2 - slot, first + (1 if slot == 0 else HALF - 2))):
-            dk, dv, dq = pairs(
-                pool_ref[0, where], pool_ref[1, where], q2, do2, lse, delta, okay if n == slot else None
-            )
-            near_ref[0, j + n] += dk
-            near_ref[1, j + n] += dv
-            dq_ref[j] += dq
+        made.append(pairs(pool_ref[0, outer], pool_ref[1, outer], q2, do2, lse, delta, okay))
+    for j, met, (dk, dv, dq) in ((0, 0, made[0]), (HALF - 1, NEAR - 1, made[1])):
+        near_ref[0, met] += dk
+        near_ref[1, met] += dv
+        dq_ref[j] += dq
 
     def near_to(n):
         for kind in range(2):
@@ -329,31 +338,35 @@
 
     terms_to(chunks, ENTRIES, NEAR).start()
 
-    def random(j):
-        q, do, lse, delta = block(j)
-        which = []
-        for r in range(RANDOM):
-            named = named_ref[j, r]
-            which.append(jnp.where(named // PLACES == s, named % PLACES, PLACES + named // PLACES))
-        keys = jnp.concatenate([pool_ref[0, w] for w in which], axis=0)
-        values = jnp.concatenate([pool_ref[1, w] for w in which], axis=0)
-        dk, dv, dq = pairs(
-            keys, values, jnp.concatenate(q, axis=0), jnp.concatenate(do, axis=0), lse, delta
-        )
-        at = pl.ds(RANDOM * j, RANDOM)
-        terms_ref[0, at] = dk.astype(BF16).reshape(RANDOM, BLOCK, FEATURES)
-        terms_ref[1, at] = dv.astype(BF16).reshape(RANDOM, BLOCK, FEATURES)
-        dq = (dq_ref[j] + dq) * SCALE
-        for i in range(2):
-            gq_ref[j, :, FEATURES * i : FEATURES * (i + 1)] = dq[BLOCK * i : BLOCK * (i + 1)].astype(BF16)
-        send(gq_ref.at[j], columns(gq_out, p_me, 2 * FEATURES), s_gq, r_gq, s, first + j, j == p_me)
-        per = CHUNK // RANDOM
-
-        @pl.when(j % per == per - 1)
+    def random(n):
+        made = []
+        for j in (2 * n, 2 * n + 1):
+            q, do, lse, delta = block(j)
+            which = []
+            for r in range(RANDOM):
+                named = named_ref[j, r]
+                which.append(jnp.where(named // PLACES == s, named % PLACES, PLACES + named // PLACES))
+            keys = jnp.concatenate([pool_ref[0, w] for w in which], axis=0)
+            values = jnp.concatenate([pool_ref[1, w] for w in which], axis=0)
+            dk, dv, dq = pairs(
+                keys, values, jnp.concatenate(q, axis=0), jnp.concatenate(do, axis=0), lse, delta
+            )
+            made.append((j, dk, dv, (dq_ref[j] + dq) * SCALE))
+        for j, dk, dv, dq in made:
+            at = pl.ds(RANDOM * j, RANDOM)
+            terms_ref[0, at] = dk.astype(BF16).reshape(RANDOM, BLOCK, FEATURES)
+            terms_ref[1, at] = dv.astype(BF16).reshape(RANDOM, BLOCK, FEATURES)
+            for i in range(2):
+                gq_ref[j, :, FEATURES * i : FEATURES * (i + 1)] = dq[BLOCK * i : BLOCK * (i + 1)].astype(BF16)
+        for j, *_ in made:
+            send(gq_ref.at[j], gq_out.at[p_me], s_gq, r_gq, s, first + j, j == p_me)
+        per = CHUNK // RANDOM // 2
+
+        @pl.when(n % per == per - 1)
         def _():
-            terms_to(j // per, j // per * CHUNK, CHUNK).start()
-
-    loop(HALF, random)
+            terms_to(n // per, n // per * CHUNK, CHUNK).start()
+
+    loop(HALF // 2, random)
     for n in range(chunks):
         terms_to(n, n * CHUNK, CHUNK).wait()
     terms_to(chunks, ENTRIES, NEAR).wait()
@@ -361,7 +374,7 @@
     def back_to(t, place):
         e = entry_ref[t]
         out_ref[t] = (terms_ref[core, e].astype(F32) + got_ref[e].astype(F32)).astype(BF16)
-        remote(out_ref.at[t], back_ref.at[s], s_back, r_back, t, place).start()
+        remote(out_ref.at[t], back_ref.at[s], s_back, r_back.at[s], t, place).start()
 
     far_peers(s, u, back_to)
 
@@ -381,9 +394,9 @@
         chain_ref[n] = both(n) + chain_ref[before_ref[n]]
 
     loop(ENTRIES, link)
-    wait(back_ref.at[rest], r_back)
 
     def link_back(t):
+        wait(back_ref.at[t], r_back.at[t])
         chain_ref[ENTRIES + t] = back_ref[t].astype(F32) + chain_ref[before_ref[ENTRIES + t]]
 
     others(SPANS, s, link_back)
@@ -424,14 +437,7 @@
 
         loop(each, rows_to)
     wait(mem_out, r_out)
-    for n in range(2):
-        mk_out[ROWS * n : ROWS * (n + 1), :] = mem_out[n]
-        mv_out[ROWS * n : ROWS * (n + 1), :] = mem_out[2 + n]
     wait(rows_ref, r_rows)
-    for head_id in range(KEY_HEADS):
-        cols = slice(FEATURES * head_id, FEATURES * (head_id + 1))
-        dk_ref[:, cols] = rows_ref[2 * head_id].astype(F32)
-        dv_ref[:, cols] = rows_ref[2 * head_id + 1].astype(F32)
     wait(gq_out, r_gq)
     wait(rows_out.at[pl.ds(0, HALF - 1)], s_rows)
     wait(gq_ref.at[pl.ds(0, HALF - 1)], s_gq)
@@ -449,7 +455,7 @@
     wait(own_ref.at[mine], s_z)
     wait(own_ref.at[mine], s_core.at[0])
     onward.wait_send()
-    onward_far.wait_send()
+    wait(far_ref.at[rest], s_core.at[2])
     wait(qh_ref.at[pl.ds(0, HALF - 1)], s_q)
     wait(doh_ref.at[pl.ds(0, HALF - 1)], s_do)
     for z in range(2):
@@ -483,10 +489,8 @@
     return pl.pallas_call(
         attend,
         in_specs=[SMEM] * 5 + hbm(8),
-        out_specs=hbm(1) + vmem(4),
-        out_shape=[shape(BLOCK, QUERY_HEADS * FEATURES)]
-        + [shape(BLOCK, KEY_HEADS * FEATURES, dtype=F32)] * 2
-        + [shape(BLOCK, FEATURES, dtype=F32)] * 2,
+        out_specs=hbm(1) + vmem(2),
+        out_shape=[shape(*wide), shape(HALF, *tile), shape(4, ROWS, FEATURES, dtype=F32)],
         scratch_shapes=[
             pltpu.VMEM(wide, BF16),
             pltpu.VMEM((LINKS + 1,) + tile, F32),
@@ -495,10 +499,8 @@
             pltpu.VMEM((HALF,) + tile, BF16),
             pltpu.VMEM((HALF,) + tile, BF16),
             pltpu.VMEM((HALF,) + tile, BF16),
-            pltpu.VMEM((HALF,) + tile, BF16),
             pltpu.VMEM((RINGS, ROWS, FEATURES), F32),
             pltpu.VMEM((ROWS, FEATURES), F32),
-            pltpu.VMEM((4, ROWS, FEATURES), F32),
             pltpu.VMEM(wide, BF16),
             pltpu.VMEM(wide, BF16),
             pltpu.VMEM((PLACES,) + tile, BF16),
@@ -515,13 +517,52 @@
             pltpu.VMEM((PARTS, ROWS, FEATURES), F32),
             pltpu.VMEM((PARTS, ROWS, FEATURES), F32),
             one, DMA((YS,)), one, DMA((HALF,)), one, DMA((HALF,)), one, one,
-            DMA((3,)), DMA((3,)), DMA((3,)), one, one, one, one,
+            DMA((3,)), DMA((3,)), DMA((3,)), one, DMA((SPANS,)), one, DMA((SPANS,)),
             per_kind, one, per_kind, one, DMA((5,)), DMA((5,)), one, one,
             one, one, DMA((CHUNKS,)), DMA((CHUNKS,)), one, one, one, one, DMA((PARTS,)), one,
         ],
         compiler_params=pltpu.CompilerParams(collective_id=0, has_side_effects=True),
         name="attend",
     )(sends, entries, named, before, last, q, do, k, v, lse, delta, mk, mv)
+
+
+STEPS = 4
+
+
+def finish(gq_ref, rows_ref, mem_ref, gq_out, dk_ref, dv_ref, mk_ref, mv_ref):
+    for n in range(HALF // STEPS):
+        gq_out[:, 2 * FEATURES * n : 2 * FEATURES * (n + 1)] = gq_ref[n]
+    for n in range(KEY_HEADS // STEPS):
+        cols = slice(FEATURES * n, FEATURES * (n + 1))
+        dk_ref[:, cols] = rows_ref[2 * n].astype(F32)
+        dv_ref[:, cols] = rows_ref[2 * n + 1].astype(F32)
+
+    @pl.when(pl.program_id(0) == 0)
+    def _():
+        for n in range(2):
+            mk_ref[ROWS * n : ROWS * (n + 1), :] = mem_ref[n]
+            mv_ref[ROWS * n : ROWS * (n + 1), :] = mem_ref[2 + n]
+
+
+def finish_call(gq, rows, mem):
+    def part(dims):
+        return pl.BlockSpec((dims[0] // STEPS,) + dims[1:], lambda i: (i, 0, 0))
+
+    def columns(width):
+        return pl.BlockSpec((BLOCK, width // STEPS), lambda i: (0, i))
+
+    one = pl.BlockSpec((BLOCK, FEATURES), lambda i: (0, 0))
+    wide, narrow = QUERY_HEADS * FEATURES, KEY_HEADS * FEATURES
+    return pl.pallas_call(
+        finish,
+        grid=(STEPS,),
+        in_specs=[part(gq.shape), part(rows.shape), pl.BlockSpec(mem.shape, lambda i: (0, 0, 0))],
+        out_specs=[columns(wide), columns(narrow), columns(narrow), one, one],
+        out_shape=[shape(BLOCK, wide)]
+        + [shape(BLOCK, narrow, dtype=F32)] * 2
+        + [shape(BLOCK, FEATURES, dtype=F32)] * 2,
+        name="finish",
+    )(gq, rows, mem)
 
 
 def shards(queries, keys, values, grad_out, row_lse, row_delta, pattern, memory_keys, memory_values):
@@ -550,10 +591,10 @@
     last = jnp.where(last < 0, LINKS, last)
 
     rows = (2, HALF, BLOCK)
-    return tuple(attend_call(
+    return tuple(finish_call(*attend_call(
         sends, entries, named, before, last, queries, grad_out, keys, values,
         row_lse.reshape(rows), row_delta.reshape(rows), memory_keys, memory_values,
-    ))
+    )))
 
 
 def solution(mesh):

time: 181 us -> 176 us (0.972)
  local copies, waits for them, and re-layouts: 7.57 us -> 1.64 us
    unnamed x18 -> x5, local copies, waits for them, and re-layouts: 7.11 us -> 1.17 us
    pallas_call x0 -> x1, Pallas kernels: none -> 3.89 us  [finish_call(): pl.pallas_call(finish, grid=(STEPS,), in_specs=[part(gq.shape), part(rows...]
    pallas_call x1, Pallas kernels: 170 us -> 167 us  [attend_call(): pl.pallas_call(attend, in_specs=[SMEM] * 5 + hbm(8), out_specs=hbm(1) + v...]
where the time goes in v4:
time: 176 us
  Pallas kernels  171 us (97%)
  other arithmetic  2.21 us (1%)
    pallas_call x1, Pallas kernels, attend_call(): pl.pallas_call(attend, in_specs=[SMEM] * 5 + hbm(8), out_specs=hbm(1) + v...  167 us
    pallas_call x1, Pallas kernels, finish_call(): pl.pallas_call(finish, grid=(STEPS,), in_specs=[part(gq.shape), part(rows...  3.89 us

profile of v4, /device:TPU:49, one launch (start us, length us, event | category | flops | bytes accessed | tf_op | source)
XLA Modules:
  0.0 175.8 jit_solution(16366677504488930942)
XLA Ops:
  0.7 0.0 copy-start.1
  0.7 0.7 copy-done.1
  1.4 0.1 constant_dynamic-slice_fusion
  1.4 0.1 and.59
  1.5 0.1 and.60
  1.6 0.1 copy.18.named_ref
  1.7 0.0 copy-start
  1.7 0.1 reduce_sum.26
  1.8 0.1 reduce_sum.27
  1.9 0.4 copy-done
  2.3 0.1 reshape.51
  2.4 0.1 copy.17
  2.5 0.1 select_reduce_fusion.2
  2.6 0.5 compare_select_fusion.2
  3.1 0.1 pad_add_fusion
  3.2 0.2 select_reduce_fusion
  3.4 0.1 select_reduce_fusion.1
  3.5 0.5 compare_select_fusion.last_ref
  4.0 0.5 compare_select_fusion.1.before_ref
  4.5 167.3 %attend.1 = (bf16[16,128,256]{2,1,0:T(8,128)(2,1)}, bf16[16,128,128]{2,1,0:T(8,128)(2,1)}, f32[4,64,128]{2,1,0:T(8,128)}) custom-call(s32[24]{0:T(128)} %get-tuple-element.12.send_ref, s32[24]{0:T(128)} %get-tuple-element.15.entry_ref, s32[16,2]{1,0:T(8,128)} %copy-done, s32[56]{0:T(128)} %compare_select_fusion.1.before_ref, s32[32]{0:T(128)} %compare_select_fusion.last_ref, ...), custom_call_target="tpu_custom_call" | custom-call | tf_op jit(solution)/shard_map/attend/pallas_call | solution.py:489
  171.9 3.9 %finish.1 = (bf16[128,4096]{1,0:T(8,128)(2,1)}, f32[128,1024]{1,0:T(8,128)}, f32[128,1024]{1,0:T(8,128)}, f32[128,128]{1,0:T(8,128)}, f32[128,128]{1,0:T(8,128)}) custom-call(bf16[16,128,256]{2,1,0:T(8,128)(2,1)} %get-tuple-element.8.gq_ref, bf16[16,128,128]{2,1,0:T(8,128)(2,1)} %get-tuple-element.9.rows_ref, f32[4,64,128]{2,1,0:T(8,128)} %get-tuple-element.10.mem_ref), custom_call_target="tpu_custom_call" | custom-call | tf_op jit(solution)/shard_map/finish/pallas_call | solution.py:556
  (4 shorter events, 0.1 us)
Async XLA Ops:
  0.7 0.7 copy-start.1
  1.7 0.6 copy-start

commit v5 on v4

--- a/solution.py
+++ b/solution.py
@@ -202,7 +202,6 @@
         send(columns(q_ref, p, 2 * FEATURES), qh_ref.at[p_me], s_q, r_q.at[p_me], s, first + p, here)
         send(columns(do_ref, p, 2 * FEATURES), doh_ref.at[p_me], s_do, r_do.at[p_me], s, first + p, here)
 
-    loop(HALF, q_to)
     near_ref[...] = jnp.zeros_like(near_ref)
     macc_ref[...] = jnp.zeros_like(macc_ref)
     for kind in range(2):
@@ -217,6 +216,8 @@
         remote(piece, piece, s_z, r_z, s, (u + HALF) % PLACES).start()
         remote(piece, pool_ref.at[core, at], s_core.at[0], r_core.at[0], s, core_peer).start()
         pltpu.make_async_copy(piece, pool_ref.at[core, at], c_own.at[0]).start()
+        q_to(2 * n)
+        q_to(2 * n + 1)
 
     loop(YS, kv_on)
     mine, theirs = pl.ds(first, HALF), pl.ds(second, HALF)
@@ -366,7 +367,16 @@
         def _():
             terms_to(n // per, n // per * CHUNK, CHUNK).start()
 
-    loop(HALF // 2, random)
+    loop(HALF // 4, random)
+    wait(parts_ref.at[pl.ds(0, PARTS - 1)], r_part)
+    parts_ref[r_me] = dmem_ref[r_me]
+    part_ref[...] = jnp.sum(parts_ref[...], axis=0)
+
+    def ring_to(r):
+        remote(part_ref, rings_ref.at[ring_me], s_ring, r_ring, *ring_peer(r)).start()
+
+    others(RINGS, ring_me, ring_to)
+    loop(HALF // 4, lambda n: random(n + HALF // 4))
     for n in range(chunks):
         terms_to(n, n * CHUNK, CHUNK).wait()
     terms_to(chunks, ENTRIES, NEAR).wait()
@@ -378,15 +388,6 @@
 
     far_peers(s, u, back_to)
 
-    wait(parts_ref.at[pl.ds(0, PARTS - 1)], r_part)
-    parts_ref[r_me] = dmem_ref[r_me]
-    part_ref[...] = jnp.sum(parts_ref[...], axis=0)
-
-    def ring_to(r):
-        remote(part_ref, rings_ref.at[ring_me], s_ring, r_ring, *ring_peer(r)).start()
-
-    others(RINGS, ring_me, ring_to)
-
     def both(n):
         return terms_ref[core, n].astype(F32) + got_ref[n].astype(F32)
 
@@ -394,6 +395,17 @@
         chain_ref[n] = both(n) + chain_ref[before_ref[n]]
 
     loop(ENTRIES, link)
+    wait(rings_ref.at[pl.ds(0, RINGS - 1)], r_ring)
+    rings_ref[ring_me] = part_ref[...]
+    total_ref[...] = jnp.sum(rings_ref[...], axis=0)
+
+    def mem_to(r):
+        blk = part_peer(s, r)
+        send(total_ref, mem_out.at[r_me % 4], s_out.at[r], r_out, blk, head, (blk == s) & (head == u))
+
+    @pl.when(gives)
+    def _():
+        loop(PARTS, mem_to)
 
     def link_back(t):
         wait(back_ref.at[t], r_back.at[t])
@@ -413,18 +425,6 @@
         at = pl.ds(c * each, each)
         swaps.append(remote(away_ref.at[at], came_ref.at[at], s_away.at[c], r_away.at[c], s, (u + HALF) % PLACES))
         swaps[-1].start()
-
-    wait(rings_ref.at[pl.ds(0, RINGS - 1)], r_ring)
-    rings_ref[ring_me] = part_ref[...]
-    total_ref[...] = jnp.sum(rings_ref[...], axis=0)
-
-    def mem_to(r):
-        blk = part_peer(s, r)
-        send(total_ref, mem_out.at[r_me % 4], s_out.at[r], r_out, blk, head, (blk == s) & (head == u))
-
-    @pl.when(gives)
-    def _():
-        loop(PARTS, mem_to)
 
     for c in range(CHUNKS):
         swaps[c].wait_recv()

time: 176 us -> 176 us (level)
  the two profiles are of different devices: /device:TPU:49 before, /device:TPU:127 now
where the time goes in v5:
time: 176 us
  Pallas kernels  171 us (97%)
  other arithmetic  2.21 us (1%)
    pallas_call x1, Pallas kernels, attend_call(): pl.pallas_call(attend, in_specs=[SMEM] * 5 + hbm(8), out_specs=hbm(1) + v...  167 us
    pallas_call x1, Pallas kernels, finish_call(): pl.pallas_call(finish, grid=(STEPS,), in_specs=[part(gq.shape), part(rows...  3.89 us

profile of v5, /device:TPU:127, one launch (start us, length us, event | category | flops | bytes accessed | tf_op | source)
XLA Modules:
  0.0 175.7 jit_solution(17308997485986905805)
XLA Ops:
  0.7 0.0 copy-start.1
  0.7 0.7 copy-done.1
  1.4 0.1 constant_dynamic-slice_fusion
  1.4 0.1 and.59
  1.5 0.1 and.60
  1.6 0.1 copy.18.named_ref
  1.7 0.0 copy-start
  1.7 0.1 reduce_sum.26
  1.8 0.1 reduce_sum.27
  1.9 0.4 copy-done
  2.3 0.1 reshape.51
  2.4 0.1 copy.17
  2.5 0.1 select_reduce_fusion.2
  2.6 0.5 compare_select_fusion.2
  3.1 0.1 pad_add_fusion
  3.2 0.2 select_reduce_fusion
  3.4 0.1 select_reduce_fusion.1
  3.5 0.5 compare_select_fusion.last_ref
  4.0 0.5 compare_select_fusion.1.before_ref
  4.5 167.2 %attend.1 = (bf16[16,128,256]{2,1,0:T(8,128)(2,1)}, bf16[16,128,128]{2,1,0:T(8,128)(2,1)}, f32[4,64,128]{2,1,0:T(8,128)}) custom-call(s32[24]{0:T(128)} %get-tuple-element.12.send_ref, s32[24]{0:T(128)} %get-tuple-element.15.entry_ref, s32[16,2]{1,0:T(8,128)} %copy-done, s32[56]{0:T(128)} %compare_select_fusion.1.before_ref, s32[32]{0:T(128)} %compare_select_fusion.last_ref, ...), custom_call_target="tpu_custom_call" | custom-call | tf_op jit(solution)/shard_map/attend/pallas_call | solution.py:489
  171.8 3.9 %finish.1 = (bf16[128,4096]{1,0:T(8,128)(2,1)}, f32[128,1024]{1,0:T(8,128)}, f32[128,1024]{1,0:T(8,128)}, f32[128,128]{1,0:T(8,128)}, f32[128,128]{1,0:T(8,128)}) custom-call(bf16[16,128,256]{2,1,0:T(8,128)(2,1)} %get-tuple-element.8.gq_ref, bf16[16,128,128]{2,1,0:T(8,128)(2,1)} %get-tuple-element.9.rows_ref, f32[4,64,128]{2,1,0:T(8,128)} %get-tuple-element.10.mem_ref), custom_call_target="tpu_custom_call" | custom-call | tf_op jit(solution)/shard_map/finish/pallas_call | solution.py:556
  (4 shorter events, 0.1 us)
Async XLA Ops:
  0.7 0.7 copy-start.1
  1.7 0.6 copy-start
